TPU v7x, 32 devices: a whole 2x2x4 slice. The times are simulated.
32 devices in a mesh: depth: 4 (over y, x), col: 8 (over z, core).
Axes of the slice: x: 2, y: 2, z: 4, core: 2. Of those that a mesh axis runs over, the one named last changes fastest.
Arguments:
- raw_views: bfloat16 [8, 32, 8, 1024], P('depth', None, None, 'col'), may hold values from -48 to 48
- feat_weight: bfloat16 [9, 32, 32], replicated, may hold values from -0.375 to 0.375
- shifts: int32 [8, 96], replicated, may hold values from 0 to 127, as said below
- frame_range: int32 [8, 2], replicated, may hold values from 0 to 1024, as said below
- cost_weight: bfloat16 [27, 8, 32], replicated, may hold values from -0.21875 to 0.21875
- mid_weight: bfloat16 [27, 8, 8], replicated, may hold values from -0.4375 to 0.4375
- final_weight: bfloat16 [27, 8], replicated, may hold values from -17 to 17
Outputs:
- estimate: float32 [8, 1024], P(None, 'col')
Inputs may be any that keep to these rules, and one draw needn't show every extreme that they name: `shifts`: shifts of view 0 are all zero; the largest shift is exactly 127. `frame_range`: row v holds the first and one past the last valid column of view v, the first below the second; view 0 is valid over all 1024 columns.
All inputs are finite; a program needn't handle non-finite values.
Results may differ from a plain program's by a relative error of at most 0.007.
The roundings to bfloat16 on the way count: a program that leaves them out, or rounds other values in their place, can miss the bound.
Values may be sent and summed in bfloat16 or wider, within the bound.
A program may use at most 64 MiB of HBM per device.

v0:
```python
import functools
import jax
import jax.numpy as jnp
from jax import lax
from jax.experimental import pallas as pl
from jax.experimental.pallas import tpu as pltpu
from jax.sharding import PartitionSpec as P

norm_eps = 1e-05
LANES = 128
ROWS = 8
f32 = jnp.float32
bf16 = jnp.bfloat16
MESH = pl.DeviceIdType.MESH
vmem = pl.BlockSpec(memory_space=pltpu.VMEM)
smem = pl.BlockSpec(memory_space=pltpu.SMEM)


def dot(a, b):
    return jnp.dot(a, b, preferred_element_type=f32)


def iota(shape, dim):
    return lax.broadcasted_iota(jnp.int32, shape, dim)


def remote(src, dst, send, recv, depth, col):
    return pltpu.make_async_remote_copy(
        src_ref=src,
        dst_ref=dst,
        send_sem=send,
        recv_sem=recv,
        device_id=(depth, col),
        device_id_type=MESH,
    )


def tree_sum(parts):
    while len(parts) > 1:
        paired = [a + b for a, b in zip(parts[::2], parts[1::2])]
        parts = paired + parts[len(paired) * 2 :]
    return parts[0]


def spread_rows(table):
    pieces = [
        jnp.broadcast_to(table[o : o + 1], (ROWS, table.shape[1])) for o in range(table.shape[0])
    ]
    return jnp.concatenate(pieces, axis=0)


def expand(weight_ref, table_ref):
    wide = table_ref.shape[1]
    spread = iota((wide // ROWS, wide), 1) // ROWS == iota((wide // ROWS, wide), 0)
    spread = jnp.where(spread, 1.0, 0.0).astype(bf16)
    if len(weight_ref.shape) == 2:
        table_ref[...] = dot(weight_ref[...], spread)
        return
    taps, count, _ = weight_ref.shape
    for tap in range(taps):
        table_ref[tap * count : (tap + 1) * count, :] = dot(weight_ref[tap], spread)


def row_bands(width):
    out_row = iota((ROWS, width), 0)
    in_row = lax.rem(iota((ROWS, width), 1), ROWS)
    return [in_row - out_row + 1 == b for b in range(3)]


def banded(table_ref, count, first, step, bands):
    picked = [table_ref[pl.ds((first + step * b) * count, count), :] for b in range(3)]
    pieces = []
    for o in range(count):
        block = jnp.zeros(bands[0].shape, f32)
        for b in range(3):
            block = jnp.where(bands[b], jnp.broadcast_to(picked[b][o : o + 1], block.shape), block)
        pieces.append(block)
    return jnp.concatenate(pieces, axis=0) if count > 1 else pieces[0]


def build_conv(table_ref, count, wide, mat_ref):
    bands = row_bands(wide)
    high = count * ROWS
    for a in range(3):
        for e in range(3):
            block = banded(table_ref, count, 9 * a + e, 3, bands)
            mat_ref[e * high : (e + 1) * high, a * wide : (a + 1) * wide] = block.astype(
                mat_ref.dtype
            )


def feature_stage(
    depths, cols, ready, raw_views, feat_weight, cost_weight, mid_weight, final_weight, own, left, right,
    cost_mat, mid_mat, final_mat, raw, table, cost_table, mid_table, final_table, raw_left, raw_right,
    mat, s_raw, r_raw, s_dep, r_dep,
    s_right, r_right, s_left, r_left
):
    me, col = lax.axis_index("depth"), lax.axis_index("col")
    count, high, n = raw.shape
    channels = high // ROWS
    has_left, has_right = col > 0, col < cols - 1
    raw[...] = raw_views[...].reshape(raw.shape)
    expand(feat_weight, table)
    bands = row_bands(high)
    for e in range(3):
        mat[e * high : (e + 1) * high, :] = banded(table, channels, e, 3, bands).astype(bf16)
    ready()

    def edge_right():
        return remote(
            raw.at[:, :, n - LANES : n], raw_left, s_raw.at[0], r_raw.at[0], me, col + 1
        )

    def edge_left():
        return remote(raw.at[:, :, 0:LANES], raw_right, s_raw.at[1], r_raw.at[1], me, col - 1)

    pl.when(has_right)(lambda: edge_right().start())
    pl.when(has_left)(lambda: edge_left().start())
    for weight, spread, built in (
        (cost_weight, cost_table, cost_mat),
        (mid_weight, mid_table, mid_mat),
        (final_weight, final_table, final_mat),
    ):
        expand(weight, spread)
        build_conv(spread, built.shape[0] // (3 * ROWS), built.shape[1] // 3, built)
    pl.when(has_left)(lambda: edge_right().wait_recv())
    pl.when(has_right)(lambda: edge_left().wait_recv())

    for v in range(count):
        before = jnp.where(has_left, raw_left[v].astype(f32), 0.0).astype(bf16)
        after = jnp.where(has_right, raw_right[v].astype(f32), 0.0).astype(bf16)
        wide = jnp.concatenate([before, raw[v], after], axis=1)
        total = None
        for e in range(3):
            part = dot(mat[e * high : (e + 1) * high, :], wide)
            part = pltpu.roll(part, (1 - e) % part.shape[1], 1)[:, LANES : LANES + n]
            total = part if total is None else total + part
        own[me * count + v] = total.astype(bf16)

    def to_depth(k, slot):
        part = pl.ds(slot * count, count)
        return remote(
            own.at[part], own.at[part], s_dep.at[k], r_dep.at[slot], lax.rem(me + k, depths), col
        )

    def to_right(k, slot):
        part = pl.ds(slot * count, count)
        return remote(
            own.at[part, :, n - LANES : n], left.at[part], s_right.at[k], r_right.at[slot], me, col + 1
        )

    def to_left(k, slot):
        part = pl.ds(slot * count, count)
        return remote(
            own.at[part, :, 0:LANES], right.at[part], s_left.at[k], r_left.at[slot], me, col - 1
        )

    for k in range(1, depths):
        to_depth(k, me).start()
    for k in range(depths):
        slot = lax.rem(me + k, depths)
        if k:
            to_depth(k, slot).wait_recv()
        pl.when(has_right)(lambda: to_right(k, slot).start())
        pl.when(has_left)(lambda: to_left(k, slot).start())
    for k in range(1, depths):
        to_depth(k, me).wait_send()
    pl.when(has_right)(lambda: edge_right().wait_send())
    pl.when(has_left)(lambda: edge_left().wait_send())
    for k in range(depths):
        slot = lax.rem(me + k, depths)
        pl.when(has_right)(lambda: to_right(k, slot).wait_send())
        pl.when(has_left)(lambda: to_left(k, slot).wait_send())
        pl.when(has_left)(lambda: to_right(k, slot).wait_recv())
        pl.when(has_right)(lambda: to_left(k, slot).wait_recv())


def convolve(slab, wide, mat, halo_left, halo_right, high, depth_local, out, pack_left, pack_right,
             stats):
    n = slab.shape[1]
    tiles = n // LANES
    edge_left = edge_right = None
    for a in range(3):
        w_a = mat[0:high, a * wide : (a + 1) * wide]
        w_b = mat[2 * high : 3 * high, a * wide : (a + 1) * wide]
        part_a = pltpu.roll(dot(w_a, halo_left), (LANES - a) % LANES, 1)
        part_b = pltpu.roll(dot(w_b, halo_right), (LANES - a) % LANES, 1)
        edge_left = part_a if edge_left is None else edge_left + part_a
        edge_right = part_b if edge_right is None else edge_right + part_b
    lane = iota((high, LANES), 1)
    column = iota((high, n), 1)
    half = depth_local // 2
    weights = mat[...]

    def over_tiles(x):
        return jnp.concatenate([x] * tiles, axis=1) if tiles > 1 else x

    def one_step(t, carry):
        halves = []
        for g in range(2):
            start = pl.multiple_of((t + g * half) * wide, wide)
            halves.append(slab[pl.ds(start, 3 * wide), :])
        product = dot(weights, jnp.concatenate(halves, axis=1))
        carry = list(carry)
        for g in range(2):
            d = t + g * half
            part = product[:, g * n : (g + 1) * n]
            from_left = pltpu.roll(part[0:high], 1, 1)
            from_right = pltpu.roll(part[2 * high : 3 * high], n - 1, 1)
            rim_left = over_tiles(pltpu.roll(edge_left, lax.rem(LANES - d, LANES), 1))
            rim_right = over_tiles(pltpu.roll(edge_right, LANES - 1 - d, 1))
            result = (
                jnp.where(column == 0, rim_left, from_left)
                + part[high : 2 * high]
                + jnp.where(column == n - 1, rim_right, from_right)
            )
            out[d] = result
            if stats is not None:
                carry[0] = carry[0] + result
                carry[1] = carry[1] + result * result
                carry[2] = jnp.where(lane == d, pltpu.roll(result[:, 0:LANES], d, 1), carry[2])
                carry[3] = jnp.where(
                    lane == d, pltpu.roll(result[:, n - LANES : n], d + 1, 1), carry[3]
                )
        return tuple(carry)

    if stats is None:
        lax.fori_loop(0, half, one_step, (), unroll=4)
        return
    wide_zero = jnp.zeros((high, n), f32)
    lane_zero = jnp.zeros((high, LANES), f32)
    first, second, pack_l, pack_r = lax.fori_loop(
        0, half, one_step, (wide_zero, wide_zero, lane_zero, lane_zero), unroll=2
    )
    pack_left[...] = pack_l
    pack_right[...] = pack_r

    def per_channel(x):
        x = sum(x[:, j * LANES : (j + 1) * LANES] for j in range(tiles))
        rows = [
            jnp.sum(x[o * ROWS : (o + 1) * ROWS], axis=0, keepdims=True)
            for o in range(high // ROWS)
        ]
        return jnp.concatenate(rows, axis=0)

    stats[0] = per_channel(first)
    stats[1] = per_channel(second)


def volume_stage(
    depth_total, depth_local, cols, own, left, right, shifts, frame, shift_rows, mat, out, pack_left,
    pack_right, stats, feats, slab, halo_views
):
    views, high, n = own.shape
    channels = high // ROWS
    first_depth = lax.axis_index("depth") * depth_local
    first_col = lax.axis_index("col") * n
    for v in range(views):
        for at, piece in ((0, left[v]), (LANES, own[v]), (LANES + n, right[v])):
            c = first_col - LANES + at + iota(piece.shape, 1)
            seen = (c >= frame[v, 0]) & (c < frame[v, 1])
            feats[v, :, at : at + piece.shape[1]] = jnp.where(seen, piece, jnp.zeros_like(piece))
    lane = iota((ROWS, LANES), 1)
    pair_lane = iota((2 * ROWS, LANES), 1)

    def one_depth(step, _):
        depth = first_depth + step - 1
        valid = (depth >= 0) & (depth < depth_total)
        clipped = jnp.clip(depth, 0, depth_total - 1)
        moves = [shifts[v, clipped] for v in range(views)]
        for j in range(n // LANES):
            x = first_col + j * LANES + lane
            wraps = []
            tally = jnp.zeros((ROWS, LANES), f32)
            for v in range(views):
                c = x - moves[v]
                mask = (c >= frame[v, 0]) & (c < frame[v, 1])
                tally = tally + jnp.where(mask, 1.0, 0.0)
                wraps.append(pair_lane < moves[v])
            scale = 1.0 / tally
            absent = views - tally
            last_scale = jnp.where(valid, scale, 0.0)
            scale, absent, last_scale = [
                jnp.concatenate([part, part], axis=0) for part in (scale, absent, last_scale)
            ]

            def one_pair(pair, _):
                rows = pl.ds(pl.multiple_of(pair * 2 * ROWS, 2 * ROWS), 2 * ROWS)
                vals = []
                for v in range(views):
                    value = feats[v, rows, (j + 1) * LANES : (j + 2) * LANES]
                    if v:
                        behind = feats[v, rows, j * LANES : (j + 1) * LANES]
                        value = jnp.where(
                            wraps[v],
                            pltpu.roll(behind, moves[v], 1),
                            pltpu.roll(value, moves[v], 1),
                        )
                    vals.append(value.astype(f32))
                average = tree_sum(vals) * scale
                square = tree_sum([(value - average) * (value - average) for value in vals])
                square = jnp.maximum(square - absent * (average * average), 0.0) * last_scale
                where_to = pl.ds(pl.multiple_of(step * high + pair * 2 * ROWS, 2 * ROWS), 2 * ROWS)
                slab[where_to, j * LANES : (j + 1) * LANES] = square.astype(bf16)
                return _

            lax.fori_loop(0, channels // 2, one_pair, 0, unroll=True)
        return _

    lax.fori_loop(0, depth_local + 2, one_depth, 0, unroll=2)

    halos = []
    padding = jnp.zeros((views, LANES - depth_total), jnp.int32)
    lane_shifts = pltpu.roll(
        jnp.concatenate([shift_rows[...], padding], axis=1),
        lax.rem(LANES + 1 - first_depth, LANES),
        1,
    )
    lane_row = iota((1, LANES), 1)
    depth_row = first_depth + lane_row - 1
    for side in range(2):
        x = first_col - 1 if side == 0 else first_col + n
        for v in range(views):
            shift_row = lane_shifts[v : v + 1, :]
            if side == 0:
                source, base = feats[v, :, 0:LANES], LANES - 1
            else:
                source, base = feats[v, :, n : n + 2 * LANES], LANES
            pick = iota((source.shape[1], LANES), 0) == base - shift_row
            halo_views[v] = dot(source, jnp.where(pick, 1.0, 0.0).astype(bf16))
        tally = jnp.zeros((1, LANES), f32)
        for v in range(views):
            c = x - lane_shifts[v : v + 1, :]
            tally = tally + jnp.where((c >= frame[v, 0]) & (c < frame[v, 1]), 1.0, 0.0)
        scale = 1.0 / jnp.maximum(tally, 1.0)
        keep = (depth_row >= 0) & (depth_row < depth_total) & (lane_row < depth_local + 2)
        keep = keep & (x >= 0) & (x < n * cols)
        total = jnp.zeros((high, LANES), f32)
        for v in range(views):
            total = total + halo_views[v]
        average = total * scale
        square = jnp.zeros((high, LANES), f32)
        for v in range(views):
            dev = halo_views[v] - average
            square = square + dev * dev
        square = jnp.maximum(square - (views - tally) * (average * average), 0.0)
        halos.append(jnp.where(keep, square * scale, 0.0).astype(bf16))
    convolve(
        slab, high, mat, halos[0], halos[1], 8 * ROWS, depth_local, out, pack_left, pack_right, stats
    )


def exchange(
    depths, cols, voxels, conv, pack_left, pack_right, stats, slab, plane_low, plane_high, from_left,
    from_right, by_depth, by_col, s_near, r_near, s_dep, r_dep, s_col, r_col
):
    me, col = lax.axis_index("depth"), lax.axis_index("col")
    depth_local, high, n = conv.shape
    has_left, has_right = col > 0, col < cols - 1
    has_low, has_high = me > 0, me < depths - 1
    def to_depth(k, slot):
        return remote(
            stats, by_depth.at[slot], s_dep.at[k], r_dep.at[slot], lax.rem(me + k, depths), col
        )

    for k in range(1, depths):
        to_depth(k, me).start()
    near = []
    down = lambda: remote(conv.at[0], plane_high, s_near.at[0], r_near.at[0], me - 1, col)
    up = lambda: remote(
        conv.at[depth_local - 1], plane_low, s_near.at[1], r_near.at[1], me + 1, col
    )
    near.append((down, has_low, has_high))
    near.append((up, has_high, has_low))
    always = col >= 0
    for i, (dd, ok, back) in enumerate(
        ((-1, has_low, has_high), (0, always, always), (1, has_high, has_low))
    ):
        near.append(
            (
                lambda dd=dd, i=i: remote(
                    pack_right, from_left.at[1 - dd], s_near.at[2 + i], r_near.at[2 + i], me + dd, col + 1
                ),
                ok & has_right,
                back & has_left,
            )
        )
        near.append(
            (
                lambda dd=dd, i=i: remote(
                    pack_left, from_right.at[1 - dd], s_near.at[5 + i], r_near.at[5 + i], me + dd, col - 1
                ),
                ok & has_left,
                back & has_right,
            )
        )
    for copy, sends, _ in near:
        pl.when(sends)(lambda copy=copy: copy().start())

    by_depth[me] = stats[...]
    for k in range(1, depths):
        to_depth(k, lax.rem(me + k, depths)).wait_recv()
    by_col[col] = sum(by_depth[p] for p in range(depths))

    def to_col(k, slot):
        return remote(
            by_col.at[slot], by_col.at[slot], s_col.at[k], r_col.at[slot], me, lax.rem(col + k, cols)
        )

    for k in range(1, cols):
        to_col(k, col).start()
    for copy, _, receives in near:
        pl.when(receives)(lambda copy=copy: copy().wait_recv())
    for k in range(1, cols):
        to_col(k, lax.rem(col + k, cols)).wait_recv()
    sums = sum(by_col[p] for p in range(cols))
    average = jnp.sum(sums[0], axis=1, keepdims=True) / voxels
    variance = jnp.sum(sums[1], axis=1, keepdims=True) / voxels - average * average
    average = spread_rows(jnp.broadcast_to(average, (high // ROWS, LANES)))
    factor = spread_rows(jnp.broadcast_to(lax.rsqrt(variance + norm_eps), (high // ROWS, LANES)))

    def activate(x):
        return jnp.maximum((x - average) * factor, 0.0)

    def activate_plane(x):
        parts = [activate(x[:, j * LANES : (j + 1) * LANES]) for j in range(n // LANES)]
        return jnp.concatenate(parts, axis=1) if len(parts) > 1 else parts[0]

    slab[0:high, :] = jnp.where(has_low, activate_plane(plane_low[...]), 0.0).astype(bf16)
    slab[(depth_local + 1) * high : (depth_local + 2) * high, :] = jnp.where(
        has_high, activate_plane(plane_high[...]), 0.0
    ).astype(bf16)

    def one_plane(d, _):
        slab[pl.ds(pl.multiple_of((d + 1) * high, high), high), :] = activate_plane(conv[d]).astype(
            bf16
        )
        return _

    lax.fori_loop(0, depth_local, one_plane, 0, unroll=2)
    lane = iota((high, LANES), 1)
    halos = []
    for parts, ok in ((from_left, has_left), (from_right, has_right)):
        low = pltpu.roll(parts[0], LANES - (depth_local - 1), 1)
        mid = pltpu.roll(parts[1], 1, 1)
        top = pltpu.roll(parts[2], depth_local + 1, 1)
        row = jnp.where(lane == 0, low, jnp.where(lane == depth_local + 1, top, mid))
        keep = ok & (lane <= depth_local + 1)
        keep = keep & (has_low | (lane > 0)) & (has_high | (lane < depth_local + 1))
        halos.append(jnp.where(keep, activate(row), 0.0).astype(bf16))

    def finish():
        for k in range(1, depths):
            to_depth(k, me).wait_send()
        for k in range(1, cols):
            to_col(k, col).wait_send()
        for copy, sends, _ in near:
            pl.when(sends)(lambda copy=copy: copy().wait_send())

    return halos, finish


def score_stage(
    depths, cols, voxels, depth_total, conv, pack_left, pack_right, stats, mat, out, score, parts,
    s_part, r_part, slab, *rest
):
    me, col = lax.axis_index("depth"), lax.axis_index("col")
    depth_local, high, n = conv.shape
    halos, finish = exchange(
        depths, cols, voxels, conv, pack_left, pack_right, stats, slab, *rest
    )
    convolve(slab, high, mat, halos[0], halos[1], ROWS, depth_local, score, None, None, None)
    planes = [score[d] for d in range(depth_local)]
    peak = functools.reduce(jnp.maximum, planes)
    total = jnp.zeros_like(peak)
    weighted = jnp.zeros_like(peak)
    first_depth = me * depth_local
    for d in range(depth_local):
        term = jnp.exp(planes[d] - peak)
        total = total + term
        weighted = weighted + term * ((first_depth + d).astype(f32) / (depth_total - 1))
    parts[me, 0] = peak
    parts[me, 1] = total
    parts[me, 2] = weighted

    def to_depth(k, slot):
        return remote(
            parts.at[slot], parts.at[slot], s_part.at[k], r_part.at[slot], lax.rem(me + k, depths), col
        )

    for k in range(1, depths):
        to_depth(k, me).start()
    for k in range(1, depths):
        to_depth(k, lax.rem(me + k, depths)).wait_recv()
    highest = functools.reduce(jnp.maximum, [parts[p, 0] for p in range(depths)])
    total = jnp.zeros_like(highest)
    weighted = jnp.zeros_like(highest)
    for p in range(depths):
        scale = jnp.exp(parts[p, 0] - highest)
        total = total + parts[p, 1] * scale
        weighted = weighted + parts[p, 2] * scale
    out[...] = weighted / total
    finish()
    for k in range(1, depths):
        to_depth(k, me).wait_send()


def whole_kernel(groups, depths, cols, voxels, depth_total, depth_local, *refs):
    (
        raw_views, feat_weight, cost_weight, mid_weight, final_weight, shifts, frame, shift_rows, out
    ) = refs[:9]
    rest, taken = [], 9
    for size in groups:
        rest.append(refs[taken : taken + size])
        taken += size
    gathered, mats, feature_refs, volume_refs, first, second, swap_a, swap_b, score_refs = rest
    me, col = lax.axis_index("depth"), lax.axis_index("col")
    has_left, has_right = col > 0, col < cols - 1
    has_low, has_high = me > 0, me < depths - 1
    count = lambda flag: flag.astype(jnp.int32)
    barrier = pltpu.get_barrier_semaphore()

    def greet(d, c):
        pl.semaphore_signal(barrier, inc=1, device_id=(d, c), device_id_type=MESH)

    for k in range(1, depths):
        greet(lax.rem(me + k, depths), col)
    for k in range(1, cols):
        greet(me, lax.rem(col + k, cols))
    for dd, ok_d in ((-1, has_low), (1, has_high)):
        for dc, ok_c in ((-1, has_left), (1, has_right)):
            pl.when(ok_d & ok_c)(lambda dd=dd, dc=dc: greet(me + dd, col + dc))
    diagonals = (count(has_low) + count(has_high)) * (count(has_left) + count(has_right))

    def ready():
        pl.semaphore_wait(barrier, depths - 1 + cols - 1 + diagonals)

    feature_stage(
        depths, cols, ready, raw_views, feat_weight, cost_weight, mid_weight, final_weight, *gathered,
        *mats, *feature_refs
    )
    volume_stage(
        depth_total, depth_local, cols, *gathered, shifts, frame, shift_rows, mats[0], *first,
        *volume_refs
    )
    halos, finish = exchange(depths, cols, voxels, *first, *swap_a)
    high = first[0].shape[1]
    convolve(swap_a[0], high, mats[1], halos[0], halos[1], high, depth_local, *second)
    finish()
    score_stage(depths, cols, voxels, depth_total, *second, mats[2], out, *score_refs, *swap_b)


def buffer(dims, kind):
    return pltpu.VMEM(dims, kind)


def dma(n):
    return pltpu.SemaphoreType.DMA((n,))


def local(raw_views, feat_weight, shifts, frame_range, cost_weight, mid_weight, final_weight):
    view_local, channels, rows, n = raw_views.shape
    depths, cols = lax.axis_size("depth"), lax.axis_size("col")
    views, depth_total = shifts.shape
    depth_local = depth_total // depths
    high = channels * rows
    hidden = cost_weight.shape[1]
    mid_high = hidden * rows
    voxels = float(depth_total * rows * n * cols)

    gathered = [
        buffer((views, high, n), bf16),
        buffer((views, high, LANES), bf16),
        buffer((views, high, LANES), bf16),
    ]
    mats = [
        buffer((3 * mid_high, 3 * high), bf16),
        buffer((3 * mid_high, 3 * mid_high), bf16),
        buffer((3 * rows, 3 * mid_high), bf16),
    ]
    feature_refs = [
        buffer((view_local, high, n), bf16),
        buffer((9 * channels, high), f32),
        buffer((27 * hidden, high), f32),
        buffer((27 * hidden, mid_high), f32),
        buffer((27, mid_high), f32),
        buffer((view_local, high, LANES), bf16),
        buffer((view_local, high, LANES), bf16),
        buffer((3 * high, high), bf16),
        dma(2), dma(2), dma(depths), dma(depths), dma(depths), dma(depths), dma(depths), dma(depths),
    ]
    volume_refs = [
        buffer((views, high, n + 2 * LANES), bf16),
        buffer(((depth_local + 2) * high, n), bf16),
        buffer((views, high, LANES), f32),
    ]

    def conv_refs():
        return [
            buffer((depth_local, mid_high, n), f32),
            buffer((mid_high, LANES), f32),
            buffer((mid_high, LANES), f32),
            buffer((2, hidden, LANES), f32),
        ]

    def swap_refs():
        return [
            buffer(((depth_local + 2) * mid_high, n), bf16),
            buffer((mid_high, n), f32),
            buffer((mid_high, n), f32),
            buffer((3, mid_high, LANES), f32),
            buffer((3, mid_high, LANES), f32),
            buffer((depths, 2, hidden, LANES), f32),
            buffer((cols, 2, hidden, LANES), f32),
            dma(8), dma(8), dma(depths), dma(depths), dma(cols), dma(cols),
        ]

    score_refs = [
        buffer((depth_local, rows, n), f32),
        buffer((depths, 3, rows, n), f32),
        dma(depths), dma(depths),
    ]
    groups = [
        gathered, mats, feature_refs, volume_refs, conv_refs(), conv_refs(), swap_refs(), swap_refs(),
        score_refs,
    ]
    return pl.pallas_call(
        functools.partial(
            whole_kernel, [len(g) for g in groups], depths, cols, voxels, depth_total, depth_local
        ),
        out_shape=jax.ShapeDtypeStruct((rows, n), f32),
        in_specs=[vmem] * 5 + [smem] * 2 + [vmem],
        out_specs=vmem,
        scratch_shapes=[ref for g in groups for ref in g],
        compiler_params=pltpu.CompilerParams(collective_id=0, has_side_effects=True),
        name="whole",
    )(
        raw_views, feat_weight, cost_weight, mid_weight, final_weight, shifts, frame_range, shifts
    )


def solution(mesh):
    in_specs = (P("depth", None, None, "col"), P(), P(), P(), P(), P(), P())
    out_specs = P(None, "col")
    return jax.shard_map(local, mesh=mesh, in_specs=in_specs, out_specs=out_specs, check_vma=False)
```

profile of v0, /device:TPU:0, one launch (start us, length us, event | category | flops | bytes accessed | tf_op | source)
XLA Modules:
  0.0 64.6 jit_solution(1493667081762822451)
XLA Ops:
  0.0 0.0 copy-start
  0.0 1.4 %copy.10.refs_6_ = s32[8,2]{1,0:T(8,128)} copy(s32[8,2]{0,1:T(2,128)} %param.10) | data formatting | bytes 128 | tf_op args[3]
  1.4 0.0 copy-done
  1.4 0.7 %copy.9.refs_4_ = bf16[27,8]{1,0:T(8,128)(2,1)} copy(bf16[27,8]{0,1:T(8,128)(2,1)S(1)} %copy-done) | data formatting | bytes 864 | tf_op args[6]
  2.1 1.5 %copy.8.refs_3_ = bf16[27,8,8]{2,1,0:T(8,128)(2,1)} copy(bf16[27,8,8]{0,2,1:T(8,128)(2,1)} %param.12) | data formatting | bytes 6912 | tf_op args[5]
  3.5 59.8 %whole.1 = f32[8,128]{1,0:T(8,128)} custom-call(bf16[2,32,8,128]{3,2,1,0:T(8,128)(2,1)} %refs_0_.1, bf16[9,32,32]{2,1,0:T(8,128)(2,1)} %refs_1_.1, bf16[27,8,32]{2,1,0:T(8,128)(2,1)} %refs_2_.1, bf16[27,8,8]{2,1,0:T(8,128)(2,1)} %copy.8.refs_3_, bf16[27,8]{1,0:T(8,128)(2,1)} %copy.9.refs_4_, s32[8,96]{1,0:T(8,128)} %refs_7_.1, s32[8,2]{1,0:T(8,128)} %copy.10.refs_6_, ...), custom_call_target="tpu_custom_call" | custom-call | tf_op jit(solution)/shard_map/whole/pallas_call | solution.py:627
  63.3 1.3 %copy.12 = f32[8,128]{1,0:T(8,128)} copy(f32[8,128]{1,0:T(8,128)} %whole.1) | data formatting | bytes 8192
Async XLA Ops:
  0.0 1.4 %copy-start = (bf16[27,8]{0,1:T(8,128)(2,1)S(1)}, bf16[27,8]{0,1:T(8,128)(2,1)}, u32[]{:S(2)}) copy-start(bf16[27,8]{0,1:T(8,128)(2,1)} %param.13) | copy-start | bytes 1300
where the time goes:
time: 64.9 us; the launch traced here: 64.6 us
  Pallas kernels  59.8 us (92%)
  local copies, waits for them, and re-layouts  4.8 us (7%)
    pallas_call x1, Pallas kernels, local(): pl.pallas_call(functools.partial(whole_kernel, [len(g) for g in groups],...  59.8 us
    unnamed x6, local copies, waits for them, and re-layouts  4.8 us

commit v1 on v0

--- a/solution.py
+++ b/solution.py
@@ -49,16 +49,18 @@
     return jnp.concatenate(pieces, axis=0)
 
 
-def expand(weight_ref, table_ref):
-    wide = table_ref.shape[1]
+def expand(weight_ref, table_ref, taps_last):
+    wide = table_ref.shape[-1]
     spread = iota((wide // ROWS, wide), 1) // ROWS == iota((wide // ROWS, wide), 0)
     spread = jnp.where(spread, 1.0, 0.0).astype(bf16)
-    if len(weight_ref.shape) == 2:
-        table_ref[...] = dot(weight_ref[...], spread)
+    if taps_last:
+        for o in range(weight_ref.shape[0]):
+            table_ref[o] = lax.dot_general(
+                weight_ref[o], spread, (((0,), (0,)), ((), ())), preferred_element_type=f32
+            )
         return
-    taps, count, _ = weight_ref.shape
-    for tap in range(taps):
-        table_ref[tap * count : (tap + 1) * count, :] = dot(weight_ref[tap], spread)
+    for tap in range(weight_ref.shape[0]):
+        table_ref[tap] = dot(weight_ref[tap], spread)
 
 
 def row_bands(width):
@@ -67,23 +69,24 @@
     return [in_row - out_row + 1 == b for b in range(3)]
 
 
-def banded(table_ref, count, first, step, bands):
-    picked = [table_ref[pl.ds((first + step * b) * count, count), :] for b in range(3)]
+def banded(table_ref, count, first, step, bands, taps_last):
     pieces = []
     for o in range(count):
         block = jnp.zeros(bands[0].shape, f32)
         for b in range(3):
-            block = jnp.where(bands[b], jnp.broadcast_to(picked[b][o : o + 1], block.shape), block)
+            tap = first + step * b
+            row = table_ref[o, tap : tap + 1, :] if taps_last else table_ref[tap, o : o + 1, :]
+            block = jnp.where(bands[b], jnp.broadcast_to(row, block.shape), block)
         pieces.append(block)
     return jnp.concatenate(pieces, axis=0) if count > 1 else pieces[0]
 
 
-def build_conv(table_ref, count, wide, mat_ref):
+def build_conv(table_ref, count, wide, mat_ref, taps_last):
     bands = row_bands(wide)
     high = count * ROWS
     for a in range(3):
         for e in range(3):
-            block = banded(table_ref, count, 9 * a + e, 3, bands)
+            block = banded(table_ref, count, 9 * a + e, 3, bands, taps_last)
             mat_ref[e * high : (e + 1) * high, a * wide : (a + 1) * wide] = block.astype(
                 mat_ref.dtype
             )
@@ -91,7 +94,7 @@
 
 def feature_stage(
     depths, cols, ready, raw_views, feat_weight, cost_weight, mid_weight, final_weight, own, left, right,
-    cost_mat, mid_mat, final_mat, raw, table, cost_table, mid_table, final_table, raw_left, raw_right,
+    edge, cost_mat, mid_mat, final_mat, raw, table, cost_table, mid_table, final_table, raw_left, raw_right,
     mat, s_raw, r_raw, s_dep, r_dep,
     s_right, r_right, s_left, r_left
 ):
@@ -100,10 +103,12 @@
     channels = high // ROWS
     has_left, has_right = col > 0, col < cols - 1
     raw[...] = raw_views[...].reshape(raw.shape)
-    expand(feat_weight, table)
+    expand(feat_weight, table, False)
     bands = row_bands(high)
     for e in range(3):
-        mat[e * high : (e + 1) * high, :] = banded(table, channels, e, 3, bands).astype(bf16)
+        mat[e * high : (e + 1) * high, :] = banded(
+            table, channels, e, 3, bands, False
+        ).astype(bf16)
     ready()
 
     def edge_right():
@@ -116,13 +121,13 @@
 
     pl.when(has_right)(lambda: edge_right().start())
     pl.when(has_left)(lambda: edge_left().start())
-    for weight, spread, built in (
-        (cost_weight, cost_table, cost_mat),
-        (mid_weight, mid_table, mid_mat),
-        (final_weight, final_table, final_mat),
+    for weight, spread, built, taps_last in (
+        (cost_weight, cost_table, cost_mat, False),
+        (mid_weight, mid_table, mid_mat, True),
+        (final_weight, final_table, final_mat, True),
     ):
-        expand(weight, spread)
-        build_conv(spread, built.shape[0] // (3 * ROWS), built.shape[1] // 3, built)
+        expand(weight, spread, taps_last)
+        build_conv(spread, built.shape[0] // (3 * ROWS), built.shape[1] // 3, built, taps_last)
     pl.when(has_left)(lambda: edge_right().wait_recv())
     pl.when(has_right)(lambda: edge_left().wait_recv())
 
@@ -149,11 +154,8 @@
             own.at[part, :, n - LANES : n], left.at[part], s_right.at[k], r_right.at[slot], me, col + 1
         )
 
-    def to_left(k, slot):
-        part = pl.ds(slot * count, count)
-        return remote(
-            own.at[part, :, 0:LANES], right.at[part], s_left.at[k], r_left.at[slot], me, col - 1
-        )
+    def to_left():
+        return remote(edge, right, s_left.at[0], r_left.at[0], me, col - 1)
 
     for k in range(1, depths):
         to_depth(k, me).start()
@@ -162,7 +164,13 @@
         if k:
             to_depth(k, slot).wait_recv()
         pl.when(has_right)(lambda: to_right(k, slot).start())
-        pl.when(has_left)(lambda: to_left(k, slot).start())
+    lane = iota((high, LANES), 1)
+    packed = jnp.zeros((high, LANES), bf16)
+    for v in range(depths * count):
+        first = own[v, :, 0:LANES]
+        packed = jnp.where(lane == v, pltpu.roll(first, v, 1) if v else first, packed)
+    edge[...] = packed
+    pl.when(has_left)(lambda: to_left().start())
     for k in range(1, depths):
         to_depth(k, me).wait_send()
     pl.when(has_right)(lambda: edge_right().wait_send())
@@ -170,9 +178,9 @@
     for k in range(depths):
         slot = lax.rem(me + k, depths)
         pl.when(has_right)(lambda: to_right(k, slot).wait_send())
-        pl.when(has_left)(lambda: to_left(k, slot).wait_send())
         pl.when(has_left)(lambda: to_right(k, slot).wait_recv())
-        pl.when(has_right)(lambda: to_left(k, slot).wait_recv())
+    pl.when(has_left)(lambda: to_left().wait_send())
+    pl.when(has_right)(lambda: to_left().wait_recv())
 
 
 def convolve(slab, wide, mat, halo_left, halo_right, high, depth_local, out, pack_left, pack_right,
@@ -243,12 +251,16 @@
         ]
         return jnp.concatenate(rows, axis=0)
 
-    stats[0] = per_channel(first)
-    stats[1] = per_channel(second)
+    count = high // ROWS
+    spot = iota((count, LANES), 1) - iota((count, LANES), 0)
+    total = jnp.sum(per_channel(first), axis=1, keepdims=True)
+    squares = jnp.sum(per_channel(second), axis=1, keepdims=True)
+    row = jnp.where(spot == 0, total, jnp.where(spot == count, squares, 0.0))
+    stats[...] = jnp.sum(row, axis=0, keepdims=True)
 
 
 def volume_stage(
-    depth_total, depth_local, cols, own, left, right, shifts, frame, shift_rows, mat, out, pack_left,
+    depth_total, depth_local, cols, own, left, right, edge, shifts, frame, shift_rows, mat, out, pack_left,
     pack_right, stats, feats, slab, halo_views
 ):
     views, high, n = own.shape
@@ -256,9 +268,9 @@
     first_depth = lax.axis_index("depth") * depth_local
     first_col = lax.axis_index("col") * n
     for v in range(views):
-        for at, piece in ((0, left[v]), (LANES, own[v]), (LANES + n, right[v])):
+        for at, piece in ((0, left[v]), (LANES, own[v])):
             c = first_col - LANES + at + iota(piece.shape, 1)
-            seen = (c >= frame[v, 0]) & (c < frame[v, 1])
+            seen = (c >= frame[0, v]) & (c < frame[1, v])
             feats[v, :, at : at + piece.shape[1]] = jnp.where(seen, piece, jnp.zeros_like(piece))
     lane = iota((ROWS, LANES), 1)
     pair_lane = iota((2 * ROWS, LANES), 1)
@@ -274,9 +286,9 @@
             tally = jnp.zeros((ROWS, LANES), f32)
             for v in range(views):
                 c = x - moves[v]
-                mask = (c >= frame[v, 0]) & (c < frame[v, 1])
+                mask = (c >= frame[0, v]) & (c < frame[1, v])
                 tally = tally + jnp.where(mask, 1.0, 0.0)
-                wraps.append(pair_lane < moves[v])
+                wraps.append(pair_lane >= LANES - moves[v])
             scale = 1.0 / tally
             absent = views - tally
             last_scale = jnp.where(valid, scale, 0.0)
@@ -291,11 +303,7 @@
                     value = feats[v, rows, (j + 1) * LANES : (j + 2) * LANES]
                     if v:
                         behind = feats[v, rows, j * LANES : (j + 1) * LANES]
-                        value = jnp.where(
-                            wraps[v],
-                            pltpu.roll(behind, moves[v], 1),
-                            pltpu.roll(value, moves[v], 1),
-                        )
+                        value = pltpu.roll(jnp.where(wraps[v], behind, value), moves[v], 1)
                     vals.append(value.astype(f32))
                 average = tree_sum(vals) * scale
                 square = tree_sum([(value - average) * (value - average) for value in vals])
@@ -309,6 +317,12 @@
 
     lax.fori_loop(0, depth_local + 2, one_depth, 0, unroll=2)
 
+    view_lane = iota(right.shape, 1)
+    ahead = jnp.zeros(right.shape, bf16)
+    for v in range(views):
+        c = first_col + n
+        seen = (c >= frame[0, v]) & (c < frame[1, v]) & (view_lane == v)
+        ahead = jnp.where(seen, right[...], ahead)
     halos = []
     padding = jnp.zeros((views, LANES - depth_total), jnp.int32)
     lane_shifts = pltpu.roll(
@@ -322,16 +336,21 @@
         x = first_col - 1 if side == 0 else first_col + n
         for v in range(views):
             shift_row = lane_shifts[v : v + 1, :]
+            row_id = iota((LANES, LANES), 0)
             if side == 0:
                 source, base = feats[v, :, 0:LANES], LANES - 1
             else:
-                source, base = feats[v, :, n : n + 2 * LANES], LANES
-            pick = iota((source.shape[1], LANES), 0) == base - shift_row
-            halo_views[v] = dot(source, jnp.where(pick, 1.0, 0.0).astype(bf16))
+                source, base = feats[v, :, n : n + LANES], LANES
+            pick = row_id == base - shift_row
+            found = dot(source, jnp.where(pick, 1.0, 0.0).astype(bf16))
+            if side:
+                pick = (row_id == v) & (shift_row == 0)
+                found = found + dot(ahead, jnp.where(pick, 1.0, 0.0).astype(bf16))
+            halo_views[v] = found
         tally = jnp.zeros((1, LANES), f32)
         for v in range(views):
             c = x - lane_shifts[v : v + 1, :]
-            tally = tally + jnp.where((c >= frame[v, 0]) & (c < frame[v, 1]), 1.0, 0.0)
+            tally = tally + jnp.where((c >= frame[0, v]) & (c < frame[1, v]), 1.0, 0.0)
         scale = 1.0 / jnp.maximum(tally, 1.0)
         keep = (depth_row >= 0) & (depth_row < depth_total) & (lane_row < depth_local + 2)
         keep = keep & (x >= 0) & (x < n * cols)
@@ -352,19 +371,26 @@
 
 def exchange(
     depths, cols, voxels, conv, pack_left, pack_right, stats, slab, plane_low, plane_high, from_left,
-    from_right, by_depth, by_col, s_near, r_near, s_dep, r_dep, s_col, r_col
+    from_right, others, s_near, r_near, s_all, r_all, known=None
 ):
     me, col = lax.axis_index("depth"), lax.axis_index("col")
     depth_local, high, n = conv.shape
     has_left, has_right = col > 0, col < cols - 1
     has_low, has_high = me > 0, me < depths - 1
-    def to_depth(k, slot):
+    def to_all(k):
+        kd, kc = k // cols, lax.rem(k, cols)
         return remote(
-            stats, by_depth.at[slot], s_dep.at[k], r_dep.at[slot], lax.rem(me + k, depths), col
-        )
-
-    for k in range(1, depths):
-        to_depth(k, me).start()
+            stats, others.at[k - 1], s_all.at[0], r_all.at[0], lax.rem(me + kd, depths),
+            lax.rem(col + kc, cols)
+        )
+
+    if known is not None:
+        known()
+    if depths * cols > 64:
+        lax.fori_loop(1, depths * cols, lambda k, _: (to_all(k).start(), _)[1], 0)
+    else:
+        for k in range(1, depths * cols):
+            to_all(jnp.int32(k)).start()
     near = []
     down = lambda: remote(conv.at[0], plane_high, s_near.at[0], r_near.at[0], me - 1, col)
     up = lambda: remote(
@@ -397,25 +423,19 @@
     for copy, sends, _ in near:
         pl.when(sends)(lambda copy=copy: copy().start())
 
-    by_depth[me] = stats[...]
-    for k in range(1, depths):
-        to_depth(k, lax.rem(me + k, depths)).wait_recv()
-    by_col[col] = sum(by_depth[p] for p in range(depths))
-
-    def to_col(k, slot):
-        return remote(
-            by_col.at[slot], by_col.at[slot], s_col.at[k], r_col.at[slot], me, lax.rem(col + k, cols)
-        )
-
-    for k in range(1, cols):
-        to_col(k, col).start()
     for copy, _, receives in near:
         pl.when(receives)(lambda copy=copy: copy().wait_recv())
-    for k in range(1, cols):
-        to_col(k, lax.rem(col + k, cols)).wait_recv()
-    sums = sum(by_col[p] for p in range(cols))
-    average = jnp.sum(sums[0], axis=1, keepdims=True) / voxels
-    variance = jnp.sum(sums[1], axis=1, keepdims=True) / voxels - average * average
+    everyone = remote(others, others, s_all.at[0], r_all.at[0], me, col)
+    everyone.wait_recv()
+    count = high // ROWS
+    sums = jnp.broadcast_to(jnp.sum(others[...], axis=0) + stats[...], (count, LANES))
+    spot = iota((count, LANES), 1) - iota((count, LANES), 0)
+
+    def pick(at):
+        return jnp.sum(jnp.where(spot == at, sums, 0.0), axis=1, keepdims=True) / voxels
+
+    average = pick(0)
+    variance = pick(count) - average * average
     average = spread_rows(jnp.broadcast_to(average, (high // ROWS, LANES)))
     factor = spread_rows(jnp.broadcast_to(lax.rsqrt(variance + norm_eps), (high // ROWS, LANES)))
 
@@ -450,10 +470,7 @@
         halos.append(jnp.where(keep, activate(row), 0.0).astype(bf16))
 
     def finish():
-        for k in range(1, depths):
-            to_depth(k, me).wait_send()
-        for k in range(1, cols):
-            to_col(k, col).wait_send()
+        everyone.wait_send()
         for copy, sends, _ in near:
             pl.when(sends)(lambda copy=copy: copy().wait_send())
 
@@ -513,7 +530,8 @@
     for size in groups:
         rest.append(refs[taken : taken + size])
         taken += size
-    gathered, mats, feature_refs, volume_refs, first, second, swap_a, swap_b, score_refs = rest
+    gathered, mats, feature_refs, volume_refs, first, second, swap_a, swap_b, score_refs, known = rest
+    known_sem = known[0]
     me, col = lax.axis_index("depth"), lax.axis_index("col")
     has_left, has_right = col > 0, col < cols - 1
     has_low, has_high = me > 0, me < depths - 1
@@ -534,6 +552,13 @@
 
     def ready():
         pl.semaphore_wait(barrier, depths - 1 + cols - 1 + diagonals)
+        for k in range(1, cols):
+            pl.semaphore_signal(
+                known_sem, inc=1, device_id=(me, lax.rem(col + k, cols)), device_id_type=MESH
+            )
+
+    def all_known():
+        pl.semaphore_wait(known_sem, cols - 1)
 
     feature_stage(
         depths, cols, ready, raw_views, feat_weight, cost_weight, mid_weight, final_weight, *gathered,
@@ -543,7 +568,7 @@
         depth_total, depth_local, cols, *gathered, shifts, frame, shift_rows, mats[0], *first,
         *volume_refs
     )
-    halos, finish = exchange(depths, cols, voxels, *first, *swap_a)
+    halos, finish = exchange(depths, cols, voxels, *first, *swap_a, all_known)
     high = first[0].shape[1]
     convolve(swap_a[0], high, mats[1], halos[0], halos[1], high, depth_local, *second)
     finish()
@@ -571,7 +596,8 @@
     gathered = [
         buffer((views, high, n), bf16),
         buffer((views, high, LANES), bf16),
-        buffer((views, high, LANES), bf16),
+        buffer((high, LANES), bf16),
+        buffer((high, LANES), bf16),
     ]
     mats = [
         buffer((3 * mid_high, 3 * high), bf16),
@@ -580,17 +606,17 @@
     ]
     feature_refs = [
         buffer((view_local, high, n), bf16),
-        buffer((9 * channels, high), f32),
-        buffer((27 * hidden, high), f32),
-        buffer((27 * hidden, mid_high), f32),
-        buffer((27, mid_high), f32),
+        buffer((9, channels, high), f32),
+        buffer((27, hidden, high), f32),
+        buffer((hidden, 27, mid_high), f32),
+        buffer((1, 27, mid_high), f32),
         buffer((view_local, high, LANES), bf16),
         buffer((view_local, high, LANES), bf16),
         buffer((3 * high, high), bf16),
-        dma(2), dma(2), dma(depths), dma(depths), dma(depths), dma(depths), dma(depths), dma(depths),
+        dma(2), dma(2), dma(depths), dma(depths), dma(depths), dma(depths), dma(1), dma(1),
     ]
     volume_refs = [
-        buffer((views, high, n + 2 * LANES), bf16),
+        buffer((views, high, n + LANES), bf16),
         buffer(((depth_local + 2) * high, n), bf16),
         buffer((views, high, LANES), f32),
     ]
@@ -600,7 +626,7 @@
             buffer((depth_local, mid_high, n), f32),
             buffer((mid_high, LANES), f32),
             buffer((mid_high, LANES), f32),
-            buffer((2, hidden, LANES), f32),
+            buffer((1, LANES), f32),
         ]
 
     def swap_refs():
@@ -610,9 +636,8 @@
             buffer((mid_high, n), f32),
             buffer((3, mid_high, LANES), f32),
             buffer((3, mid_high, LANES), f32),
-            buffer((depths, 2, hidden, LANES), f32),
-            buffer((cols, 2, hidden, LANES), f32),
-            dma(8), dma(8), dma(depths), dma(depths), dma(cols), dma(cols),
+            buffer((depths * cols - 1, 1, LANES), f32),
+            dma(8), dma(8), dma(1), dma(1),
         ]
 
     score_refs = [
@@ -622,7 +647,7 @@
     ]
     groups = [
         gathered, mats, feature_refs, volume_refs, conv_refs(), conv_refs(), swap_refs(), swap_refs(),
-        score_refs,
+        score_refs, [pltpu.SemaphoreType.REGULAR],
     ]
     return pl.pallas_call(
         functools.partial(
@@ -635,7 +660,8 @@
         compiler_params=pltpu.CompilerParams(collective_id=0, has_side_effects=True),
         name="whole",
     )(
-        raw_views, feat_weight, cost_weight, mid_weight, final_weight, shifts, frame_range, shifts
+        raw_views, feat_weight, cost_weight, jnp.transpose(mid_weight, (1, 2, 0)),
+        jnp.transpose(final_weight)[None], shifts, jnp.transpose(frame_range), shifts
     )
 
 

time: 64.9 us -> 56 us (0.86)
  Pallas kernels: 59.8 us -> 54.6 us
  local copies, waits for them, and re-layouts: 4.8 us -> 1.28 us
    pallas_call x1, Pallas kernels: 59.8 us -> 54.6 us  [local(): pl.pallas_call(functools.partial(whole_kernel, [len(g) for g in groups],...]
    unnamed x6 -> x1, local copies, waits for them, and re-layouts: 4.8 us -> 1.28 us
where the time goes in v1:
time: 56 us; the launch traced here: 55.9 us
  Pallas kernels  54.6 us (98%)
  local copies, waits for them, and re-layouts  1.28 us (2%)
    pallas_call x1, Pallas kernels, local(): pl.pallas_call(functools.partial(whole_kernel, [len(g) for g in groups],...  54.6 us
    unnamed x1, local copies, waits for them, and re-layouts  1.28 us

profile of v1, /device:TPU:0, one launch (start us, length us, event | category | flops | bytes accessed | tf_op | source)
XLA Modules:
  0.0 55.9 jit_solution(4100535733139328267)
XLA Ops:
  0.0 54.6 %whole.1 = f32[8,128]{1,0:T(8,128)} custom-call(bf16[2,32,8,128]{3,2,1,0:T(8,128)(2,1)} %refs_0_.1, bf16[9,32,32]{2,1,0:T(8,128)(2,1)} %refs_1_.1, bf16[27,8,32]{2,1,0:T(8,128)(2,1)} %refs_2_.1, bf16[8,8,27]{2,1,0:T(8,128)(2,1)} %bitcast.5, bf16[1,8,27]{2,1,0:T(8,128)(2,1)} %bitcast.6, s32[8,96]{1,0:T(8,128)} %refs_7_.1, s32[2,8]{1,0:T(2,128)} %bitcast.7, ...), custom_call_target="tpu_custom_call" | custom-call | tf_op jit(solution)/shard_map/whole/pallas_call | solution.py:652
  54.6 1.3 %copy.9 = f32[8,128]{1,0:T(8,128)} copy(f32[8,128]{1,0:T(8,128)} %whole.1) | data formatting | bytes 8192

commit v2 on v1

--- a/solution.py
+++ b/solution.py
@@ -92,35 +92,94 @@
             )
 
 
+def partner(me, depths, k):
+    if depths == 4:
+        return [me, me + 1 - 2 * lax.rem(me, 2), lax.rem(me + 2, 4), 3 - me][k]
+    return lax.rem(me + k, depths)
+
+
+def origin(me, depths, k):
+    return partner(me, depths, k if depths == 4 else (depths - k) % depths)
+
+
 def feature_stage(
-    depths, cols, ready, raw_views, feat_weight, cost_weight, mid_weight, final_weight, own, left, right,
-    edge, cost_mat, mid_mat, final_mat, raw, table, cost_table, mid_table, final_table, raw_left, raw_right,
-    mat, s_raw, r_raw, s_dep, r_dep,
-    s_right, r_right, s_left, r_left
+    depths, cols, ready, raw_views, feat_weight, cost_weight, mid_weight, final_weight, frame, own, left,
+    right, edge, feats, cost_mat, mid_mat, final_mat, raw, table, cost_table, mid_table, final_table,
+    rim, rim_left, rim_right, partial, mat, s_raw, r_raw, s_dep, r_dep, s_right, r_right, s_left, r_left
 ):
     me, col = lax.axis_index("depth"), lax.axis_index("col")
     count, high, n = raw.shape
+    views = depths * count
     channels = high // ROWS
     has_left, has_right = col > 0, col < cols - 1
+    first_col = col * n
+    lane = iota((high, LANES), 1)
+    half = LANES // 2
     raw[...] = raw_views[...].reshape(raw.shape)
+    packed = jnp.zeros((high, LANES), bf16)
+    for v in range(count):
+        first, last = raw[v, :, 0:LANES], raw[v, :, n - LANES : n]
+        packed = jnp.where(lane == v, pltpu.roll(first, v, 1) if v else first, packed)
+        packed = jnp.where(lane == half + v, pltpu.roll(last, half + v + 1, 1), packed)
+    rim[...] = packed
+    ready()
+
+    def edge_right():
+        return remote(rim, rim_left, s_raw.at[0], r_raw.at[0], me, col + 1)
+
+    def edge_left():
+        return remote(rim, rim_right, s_raw.at[1], r_raw.at[1], me, col - 1)
+
+    pl.when(has_right)(lambda: edge_right().start())
+    pl.when(has_left)(lambda: edge_left().start())
     expand(feat_weight, table, False)
     bands = row_bands(high)
     for e in range(3):
         mat[e * high : (e + 1) * high, :] = banded(
             table, channels, e, 3, bands, False
         ).astype(bf16)
-    ready()
-
-    def edge_right():
+    column = iota((high, n), 1)
+    for v in range(count):
+        before = pltpu.roll(dot(mat[0:high, :], raw[v]), 1, 1)
+        after = pltpu.roll(dot(mat[2 * high : 3 * high, :], raw[v]), n - 1, 1)
+        total = jnp.where(column == 0, 0.0, before) + dot(mat[high : 2 * high, :], raw[v])
+        partial[v] = total + jnp.where(column == n - 1, 0.0, after)
+    pl.when(has_left)(lambda: edge_right().wait_recv())
+    pl.when(has_right)(lambda: edge_left().wait_recv())
+    pick = has_left & (lane >= half) & (lane < half + count)
+    before = dot(mat[0:high, :], jnp.where(pick, rim_left[...].astype(f32), 0.0).astype(bf16))
+    pick = has_right & (lane < count)
+    after = dot(
+        mat[2 * high : 3 * high, :], jnp.where(pick, rim_right[...].astype(f32), 0.0).astype(bf16)
+    )
+    zero = jnp.zeros((high, n - LANES), f32)
+    for v in range(count):
+        low = jnp.where(lane == 0, pltpu.roll(before, half - v, 1), 0.0)
+        top = jnp.where(lane == LANES - 1, pltpu.roll(after, LANES - 1 - v, 1), 0.0)
+        if n > LANES:
+            low = jnp.concatenate([low, zero], axis=1)
+            top = jnp.concatenate([zero, top], axis=1)
+        own[me * count + v] = (partial[v] + low + top).astype(bf16)
+
+    def to_depth(k, j, slot):
+        v = slot * count + j
         return remote(
-            raw.at[:, :, n - LANES : n], raw_left, s_raw.at[0], r_raw.at[0], me, col + 1
+            own.at[v], own.at[v], s_dep.at[k * count + j], r_dep.at[v], partner(me, depths, k), col
         )
 
-    def edge_left():
-        return remote(raw.at[:, :, 0:LANES], raw_right, s_raw.at[1], r_raw.at[1], me, col - 1)
-
-    pl.when(has_right)(lambda: edge_right().start())
-    pl.when(has_left)(lambda: edge_left().start())
+    def to_right(v):
+        return remote(
+            own.at[v, :, n - LANES : n], left.at[v], s_right.at[v], r_right.at[v], me, col + 1
+        )
+
+    def to_left():
+        return remote(edge, right, s_left.at[0], r_left.at[0], me, col - 1)
+
+    for k in range(1, depths):
+        for j in range(count):
+            to_depth(k, j, me).start()
+    for j in range(count):
+        pl.when(has_right)(lambda j=j: to_right(me * count + j).start())
     for weight, spread, built, taps_last in (
         (cost_weight, cost_table, cost_mat, False),
         (mid_weight, mid_table, mid_mat, True),
@@ -128,62 +187,44 @@
     ):
         expand(weight, spread, taps_last)
         build_conv(spread, built.shape[0] // (3 * ROWS), built.shape[1] // 3, built, taps_last)
-    pl.when(has_left)(lambda: edge_right().wait_recv())
-    pl.when(has_right)(lambda: edge_left().wait_recv())
-
-    for v in range(count):
-        before = jnp.where(has_left, raw_left[v].astype(f32), 0.0).astype(bf16)
-        after = jnp.where(has_right, raw_right[v].astype(f32), 0.0).astype(bf16)
-        wide = jnp.concatenate([before, raw[v], after], axis=1)
-        total = None
-        for e in range(3):
-            part = dot(mat[e * high : (e + 1) * high, :], wide)
-            part = pltpu.roll(part, (1 - e) % part.shape[1], 1)[:, LANES : LANES + n]
-            total = part if total is None else total + part
-        own[me * count + v] = total.astype(bf16)
-
-    def to_depth(k, slot):
-        part = pl.ds(slot * count, count)
-        return remote(
-            own.at[part], own.at[part], s_dep.at[k], r_dep.at[slot], lax.rem(me + k, depths), col
-        )
-
-    def to_right(k, slot):
-        part = pl.ds(slot * count, count)
-        return remote(
-            own.at[part, :, n - LANES : n], left.at[part], s_right.at[k], r_right.at[slot], me, col + 1
-        )
-
-    def to_left():
-        return remote(edge, right, s_left.at[0], r_left.at[0], me, col - 1)
-
-    for k in range(1, depths):
-        to_depth(k, me).start()
-    for k in range(depths):
-        slot = lax.rem(me + k, depths)
+
+    def absorb(v, source, at, width):
+        c = first_col - LANES + at + iota((high, width), 1)
+        seen = (c >= frame[0, v]) & (c < frame[1, v])
+        feats[v, :, at : at + width] = jnp.where(seen, source[v], jnp.zeros((high, width), bf16))
+
+    order = [(k, j) for k in range(depths) for j in range(count)]
+    for k, j in order:
+        v = origin(me, depths, k) * count + j
         if k:
-            to_depth(k, slot).wait_recv()
-        pl.when(has_right)(lambda: to_right(k, slot).start())
-    lane = iota((high, LANES), 1)
+            to_depth(k, j, origin(me, depths, k)).wait_recv()
+            pl.when(has_right)(lambda v=v: to_right(v).start())
+        absorb(v, own, LANES, n)
     packed = jnp.zeros((high, LANES), bf16)
-    for v in range(depths * count):
+    for v in range(views):
         first = own[v, :, 0:LANES]
         packed = jnp.where(lane == v, pltpu.roll(first, v, 1) if v else first, packed)
     edge[...] = packed
     pl.when(has_left)(lambda: to_left().start())
-    for k in range(1, depths):
-        to_depth(k, me).wait_send()
-    pl.when(has_right)(lambda: edge_right().wait_send())
-    pl.when(has_left)(lambda: edge_left().wait_send())
-    for k in range(depths):
-        slot = lax.rem(me + k, depths)
-        pl.when(has_right)(lambda: to_right(k, slot).wait_send())
-        pl.when(has_left)(lambda: to_right(k, slot).wait_recv())
-    pl.when(has_left)(lambda: to_left().wait_send())
+    for k, j in order:
+        v = origin(me, depths, k) * count + j
+        pl.when(has_left)(lambda v=v: to_right(v).wait_recv())
+        absorb(v, left, 0, LANES)
     pl.when(has_right)(lambda: to_left().wait_recv())
 
-
-def convolve(slab, wide, mat, halo_left, halo_right, high, depth_local, out, pack_left, pack_right,
+    def finish():
+        pl.when(has_right)(lambda: edge_right().wait_send())
+        pl.when(has_left)(lambda: edge_left().wait_send())
+        for k, j in order:
+            if k:
+                to_depth(k, j, me).wait_send()
+            pl.when(has_right)(lambda k=k, j=j: to_right(k * count + j).wait_send())
+        pl.when(has_left)(lambda: to_left().wait_send())
+
+    return finish
+
+
+def convolve(slab, wide, mat, halo_left, halo_right, far, high, depth_local, out, pack_left, pack_right,
              stats):
     n = slab.shape[1]
     tiles = n // LANES
@@ -192,7 +233,7 @@
         w_a = mat[0:high, a * wide : (a + 1) * wide]
         w_b = mat[2 * high : 3 * high, a * wide : (a + 1) * wide]
         part_a = pltpu.roll(dot(w_a, halo_left), (LANES - a) % LANES, 1)
-        part_b = pltpu.roll(dot(w_b, halo_right), (LANES - a) % LANES, 1)
+        part_b = pltpu.roll(dot(w_b, halo_right), (LANES - a - far) % LANES, 1)
         edge_left = part_a if edge_left is None else edge_left + part_a
         edge_right = part_b if edge_right is None else edge_right + part_b
     lane = iota((high, LANES), 1)
@@ -260,18 +301,13 @@
 
 
 def volume_stage(
-    depth_total, depth_local, cols, own, left, right, edge, shifts, frame, shift_rows, mat, out, pack_left,
-    pack_right, stats, feats, slab, halo_views
+    depth_total, depth_local, cols, own, left, right, edge, feats, shifts, frame, shift_rows, mat, out,
+    pack_left, pack_right, stats, slab
 ):
     views, high, n = own.shape
     channels = high // ROWS
     first_depth = lax.axis_index("depth") * depth_local
     first_col = lax.axis_index("col") * n
-    for v in range(views):
-        for at, piece in ((0, left[v]), (LANES, own[v])):
-            c = first_col - LANES + at + iota(piece.shape, 1)
-            seen = (c >= frame[0, v]) & (c < frame[1, v])
-            feats[v, :, at : at + piece.shape[1]] = jnp.where(seen, piece, jnp.zeros_like(piece))
     lane = iota((ROWS, LANES), 1)
     pair_lane = iota((2 * ROWS, LANES), 1)
 
@@ -290,10 +326,9 @@
                 tally = tally + jnp.where(mask, 1.0, 0.0)
                 wraps.append(pair_lane >= LANES - moves[v])
             scale = 1.0 / tally
-            absent = views - tally
             last_scale = jnp.where(valid, scale, 0.0)
-            scale, absent, last_scale = [
-                jnp.concatenate([part, part], axis=0) for part in (scale, absent, last_scale)
+            scale, last_scale = [
+                jnp.concatenate([part, part], axis=0) for part in (scale, last_scale)
             ]
 
             def one_pair(pair, _):
@@ -305,9 +340,9 @@
                         behind = feats[v, rows, j * LANES : (j + 1) * LANES]
                         value = pltpu.roll(jnp.where(wraps[v], behind, value), moves[v], 1)
                     vals.append(value.astype(f32))
-                average = tree_sum(vals) * scale
-                square = tree_sum([(value - average) * (value - average) for value in vals])
-                square = jnp.maximum(square - absent * (average * average), 0.0) * last_scale
+                total = tree_sum(vals)
+                square = tree_sum([value * value for value in vals])
+                square = jnp.maximum(square - total * (total * scale), 0.0) * last_scale
                 where_to = pl.ds(pl.multiple_of(step * high + pair * 2 * ROWS, 2 * ROWS), 2 * ROWS)
                 slab[where_to, j * LANES : (j + 1) * LANES] = square.astype(bf16)
                 return _
@@ -323,49 +358,49 @@
         c = first_col + n
         seen = (c >= frame[0, v]) & (c < frame[1, v]) & (view_lane == v)
         ahead = jnp.where(seen, right[...], ahead)
-    halos = []
+    half = LANES // 2
     padding = jnp.zeros((views, LANES - depth_total), jnp.int32)
-    lane_shifts = pltpu.roll(
-        jnp.concatenate([shift_rows[...], padding], axis=1),
-        lax.rem(LANES + 1 - first_depth, LANES),
-        1,
-    )
+    padded = jnp.concatenate([shift_rows[...], padding], axis=1)
     lane_row = iota((1, LANES), 1)
-    depth_row = first_depth + lane_row - 1
-    for side in range(2):
-        x = first_col - 1 if side == 0 else first_col + n
-        for v in range(views):
-            shift_row = lane_shifts[v : v + 1, :]
-            row_id = iota((LANES, LANES), 0)
-            if side == 0:
-                source, base = feats[v, :, 0:LANES], LANES - 1
-            else:
-                source, base = feats[v, :, n : n + LANES], LANES
-            pick = row_id == base - shift_row
-            found = dot(source, jnp.where(pick, 1.0, 0.0).astype(bf16))
-            if side:
-                pick = (row_id == v) & (shift_row == 0)
-                found = found + dot(ahead, jnp.where(pick, 1.0, 0.0).astype(bf16))
-            halo_views[v] = found
-        tally = jnp.zeros((1, LANES), f32)
-        for v in range(views):
-            c = x - lane_shifts[v : v + 1, :]
-            tally = tally + jnp.where((c >= frame[0, v]) & (c < frame[1, v]), 1.0, 0.0)
-        scale = 1.0 / jnp.maximum(tally, 1.0)
-        keep = (depth_row >= 0) & (depth_row < depth_total) & (lane_row < depth_local + 2)
-        keep = keep & (x >= 0) & (x < n * cols)
-        total = jnp.zeros((high, LANES), f32)
-        for v in range(views):
-            total = total + halo_views[v]
-        average = total * scale
-        square = jnp.zeros((high, LANES), f32)
-        for v in range(views):
-            dev = halo_views[v] - average
-            square = square + dev * dev
-        square = jnp.maximum(square - (views - tally) * (average * average), 0.0)
-        halos.append(jnp.where(keep, square * scale, 0.0).astype(bf16))
+    far = lane_row >= half
+    step_row = jnp.where(far, lane_row - half, lane_row)
+    depth_row = first_depth + step_row - 1
+    lane_shifts = jnp.where(
+        far,
+        pltpu.roll(padded, lax.rem(LANES + half + 1 - first_depth, LANES), 1),
+        pltpu.roll(padded, lax.rem(LANES + 1 - first_depth, LANES), 1),
+    )
+    x_row = jnp.where(far, first_col + n, first_col - 1)
+    row_id = iota((n + LANES, LANES), 0)
+    base = jnp.where(far, n + LANES, LANES - 1)
+    total = jnp.zeros((high, LANES), f32)
+    squares = jnp.zeros((high, LANES), f32)
+    tally = jnp.zeros((1, LANES), f32)
+    touch = jnp.zeros((LANES, LANES), f32)
+    for v in range(views):
+        shift_row = lane_shifts[v : v + 1, :]
+        pick = row_id == base - shift_row
+        found = dot(feats[v], jnp.where(pick, 1.0, 0.0).astype(bf16))
+        total = total + found
+        squares = squares + found * found
+        c = x_row - shift_row
+        tally = tally + jnp.where((c >= frame[0, v]) & (c < frame[1, v]), 1.0, 0.0)
+        hit = far & (shift_row == 0) & (iota((LANES, LANES), 0) == v)
+        touch = jnp.where(hit, 1.0, touch)
+    touch = touch.astype(bf16)
+    wide = ahead.astype(f32) * ahead.astype(f32)
+    coarse = wide.astype(bf16)
+    fine = (wide - coarse.astype(f32)).astype(bf16)
+    total = total + dot(ahead, touch)
+    squares = squares + dot(coarse, touch) + dot(fine, touch)
+    scale = 1.0 / jnp.maximum(tally, 1.0)
+    keep = (depth_row >= 0) & (depth_row < depth_total) & (step_row < depth_local + 2)
+    keep = keep & (x_row >= 0) & (x_row < n * cols)
+    square = jnp.maximum(squares - total * (total * scale), 0.0)
+    halo = jnp.where(keep, square * scale, 0.0).astype(bf16)
     convolve(
-        slab, high, mat, halos[0], halos[1], 8 * ROWS, depth_local, out, pack_left, pack_right, stats
+        slab, high, mat, halo, halo, half, mat.shape[0] // 3, depth_local, out, pack_left, pack_right,
+        stats
     )
 
 
@@ -486,7 +521,7 @@
     halos, finish = exchange(
         depths, cols, voxels, conv, pack_left, pack_right, stats, slab, *rest
     )
-    convolve(slab, high, mat, halos[0], halos[1], ROWS, depth_local, score, None, None, None)
+    convolve(slab, high, mat, halos[0], halos[1], 0, ROWS, depth_local, score, None, None, None)
     planes = [score[d] for d in range(depth_local)]
     peak = functools.reduce(jnp.maximum, planes)
     total = jnp.zeros_like(peak)
@@ -560,9 +595,9 @@
     def all_known():
         pl.semaphore_wait(known_sem, cols - 1)
 
-    feature_stage(
-        depths, cols, ready, raw_views, feat_weight, cost_weight, mid_weight, final_weight, *gathered,
-        *mats, *feature_refs
+    sent = feature_stage(
+        depths, cols, ready, raw_views, feat_weight, cost_weight, mid_weight, final_weight, frame,
+        *gathered, *mats, *feature_refs
     )
     volume_stage(
         depth_total, depth_local, cols, *gathered, shifts, frame, shift_rows, mats[0], *first,
@@ -570,8 +605,9 @@
     )
     halos, finish = exchange(depths, cols, voxels, *first, *swap_a, all_known)
     high = first[0].shape[1]
-    convolve(swap_a[0], high, mats[1], halos[0], halos[1], high, depth_local, *second)
+    convolve(swap_a[0], high, mats[1], halos[0], halos[1], 0, high, depth_local, *second)
     finish()
+    sent()
     score_stage(depths, cols, voxels, depth_total, *second, mats[2], out, *score_refs, *swap_b)
 
 
@@ -598,6 +634,7 @@
         buffer((views, high, LANES), bf16),
         buffer((high, LANES), bf16),
         buffer((high, LANES), bf16),
+        buffer((views, high, n + LANES), bf16),
     ]
     mats = [
         buffer((3 * mid_high, 3 * high), bf16),
@@ -610,15 +647,15 @@
         buffer((27, hidden, high), f32),
         buffer((hidden, 27, mid_high), f32),
         buffer((1, 27, mid_high), f32),
-        buffer((view_local, high, LANES), bf16),
-        buffer((view_local, high, LANES), bf16),
+        buffer((high, LANES), bf16),
+        buffer((high, LANES), bf16),
+        buffer((high, LANES), bf16),
+        buffer((view_local, high, n), f32),
         buffer((3 * high, high), bf16),
-        dma(2), dma(2), dma(depths), dma(depths), dma(depths), dma(depths), dma(1), dma(1),
+        dma(2), dma(2), dma(views), dma(views), dma(views), dma(views), dma(1), dma(1),
     ]
     volume_refs = [
-        buffer((views, high, n + LANES), bf16),
         buffer(((depth_local + 2) * high, n), bf16),
-        buffer((views, high, LANES), f32),
     ]
 
     def conv_refs():

time: 56 us -> 50.8 us (0.907)
  Pallas kernels: 54.6 us -> 49.3 us
    pallas_call x1, Pallas kernels: 54.6 us -> 49.3 us  [local(): pl.pallas_call(functools.partial(whole_kernel, [len(g) for g in groups],...]
where the time goes in v2:
time: 50.8 us; the launch traced here: 50.6 us
  Pallas kernels  49.3 us (97%)
  local copies, waits for them, and re-layouts  1.28 us (3%)
    pallas_call x1, Pallas kernels, local(): pl.pallas_call(functools.partial(whole_kernel, [len(g) for g in groups],...  49.3 us
    unnamed x1, local copies, waits for them, and re-layouts  1.28 us

profile of v2, /device:TPU:0, one launch (start us, length us, event | category | flops | bytes accessed | tf_op | source)
XLA Modules:
  0.0 50.6 jit_solution(16459819014312125670)
XLA Ops:
  0.0 49.3 %whole.1 = f32[8,128]{1,0:T(8,128)} custom-call(bf16[2,32,8,128]{3,2,1,0:T(8,128)(2,1)} %refs_0_.1, bf16[9,32,32]{2,1,0:T(8,128)(2,1)} %refs_1_.1, bf16[27,8,32]{2,1,0:T(8,128)(2,1)} %refs_2_.1, bf16[8,8,27]{2,1,0:T(8,128)(2,1)} %bitcast.5, bf16[1,8,27]{2,1,0:T(8,128)(2,1)} %bitcast.6, s32[8,96]{1,0:T(8,128)} %refs_7_.1, s32[2,8]{1,0:T(2,128)} %bitcast.7, ...), custom_call_target="tpu_custom_call" | custom-call | tf_op jit(solution)/shard_map/whole/pallas_call | solution.py:689
  49.3 1.3 %copy.9 = f32[8,128]{1,0:T(8,128)} copy(f32[8,128]{1,0:T(8,128)} %whole.1) | data formatting | bytes 8192

commit v3 on v2

--- a/solution.py
+++ b/solution.py
@@ -103,7 +103,7 @@
 
 
 def feature_stage(
-    depths, cols, ready, raw_views, feat_weight, cost_weight, mid_weight, final_weight, frame, own, left,
+    depths, cols, ready, run_pass, raw_views, feat_weight, cost_weight, mid_weight, final_weight, frame, own, left,
     right, edge, feats, cost_mat, mid_mat, final_mat, raw, table, cost_table, mid_table, final_table,
     rim, rim_left, rim_right, partial, mat, s_raw, r_raw, s_dep, r_dep, s_right, r_right, s_left, r_left
 ):
@@ -161,11 +161,25 @@
             top = jnp.concatenate([zero, top], axis=1)
         own[me * count + v] = (partial[v] + low + top).astype(bf16)
 
-    def to_depth(k, j, slot):
-        v = slot * count + j
-        return remote(
-            own.at[v], own.at[v], s_dep.at[k * count + j], r_dep.at[v], partner(me, depths, k), col
-        )
+    relayed = depths == 4 and count == 2
+    at = [[origin(me, depths, k) * count + j for j in range(count)] for k in range(depths)]
+    if relayed:
+        groups = [[(0, 0), (0, 1)], [(1, 1), (2, 0)], [(1, 0), (2, 1)], [(3, 0), (3, 1)]]
+        direct = [(1, 1), (2, 0), (1, 0), (2, 1)]
+        relays = {(1, 1): 2, (2, 0): 1}
+    else:
+        groups = [[(k, j) for j in range(count)] for k in range(depths)]
+        direct = [(k, j) for k in range(1, depths) for j in range(count)]
+        relays = {}
+
+    def send(v, k, sem):
+        return remote(own.at[v], own.at[v], s_dep.at[sem], r_dep.at[v], partner(me, depths, k), col)
+
+    def relay(k, j):
+        return send(at[k][j], relays[k, j], depths * count + relays[k, j])
+
+    def to_depth(k, j):
+        return send(me * count + j, k, k * count + j)
 
     def to_right(v):
         return remote(
@@ -175,9 +189,8 @@
     def to_left():
         return remote(edge, right, s_left.at[0], r_left.at[0], me, col - 1)
 
-    for k in range(1, depths):
-        for j in range(count):
-            to_depth(k, j, me).start()
+    for k, j in direct:
+        to_depth(k, j).start()
     for j in range(count):
         pl.when(has_right)(lambda j=j: to_right(me * count + j).start())
     for weight, spread, built, taps_last in (
@@ -188,37 +201,53 @@
         expand(weight, spread, taps_last)
         build_conv(spread, built.shape[0] // (3 * ROWS), built.shape[1] // 3, built, taps_last)
 
-    def absorb(v, source, at, width):
-        c = first_col - LANES + at + iota((high, width), 1)
+    def absorb(v, source, begin, width):
+        c = first_col - LANES + begin + iota((high, width), 1)
         seen = (c >= frame[0, v]) & (c < frame[1, v])
-        feats[v, :, at : at + width] = jnp.where(seen, source[v], jnp.zeros((high, width), bf16))
-
-    order = [(k, j) for k in range(depths) for j in range(count)]
-    for k, j in order:
-        v = origin(me, depths, k) * count + j
-        if k:
-            to_depth(k, j, origin(me, depths, k)).wait_recv()
-            pl.when(has_right)(lambda v=v: to_right(v).start())
-        absorb(v, own, LANES, n)
+        feats[v, :, begin : begin + width] = jnp.where(seen, source[v], jnp.zeros((high, width), bf16))
+
+    def take(group):
+        for k, j in group:
+            v = at[k][j]
+            if k:
+                remote(own.at[v], own.at[v], s_dep.at[0], r_dep.at[v], me, col).wait_recv()
+                if (k, j) in relays:
+                    relay(k, j).start()
+                pl.when(has_right)(lambda v=v: to_right(v).start())
+        for k, j in group:
+            absorb(at[k][j], own, LANES, n)
+
+    def use(index):
+        for k, j in groups[index]:
+            v = at[k][j]
+            pl.when(has_left)(lambda v=v: to_right(v).wait_recv())
+            absorb(v, left, 0, LANES)
+        run_pass([at[k][j] for k, j in groups[index]], index == 0, index == len(groups) - 1)
+
+    take(groups[0])
+    take(groups[1])
+    use(0)
+    for group in groups[2:]:
+        take(group)
     packed = jnp.zeros((high, LANES), bf16)
     for v in range(views):
         first = own[v, :, 0:LANES]
         packed = jnp.where(lane == v, pltpu.roll(first, v, 1) if v else first, packed)
     edge[...] = packed
     pl.when(has_left)(lambda: to_left().start())
-    for k, j in order:
-        v = origin(me, depths, k) * count + j
-        pl.when(has_left)(lambda v=v: to_right(v).wait_recv())
-        absorb(v, left, 0, LANES)
+    for index in range(1, len(groups)):
+        use(index)
     pl.when(has_right)(lambda: to_left().wait_recv())
 
     def finish():
         pl.when(has_right)(lambda: edge_right().wait_send())
         pl.when(has_left)(lambda: edge_left().wait_send())
-        for k, j in order:
-            if k:
-                to_depth(k, j, me).wait_send()
-            pl.when(has_right)(lambda k=k, j=j: to_right(k * count + j).wait_send())
+        for k, j in direct:
+            to_depth(k, j).wait_send()
+        for k, j in relays:
+            relay(k, j).wait_send()
+        for v in range(views):
+            pl.when(has_right)(lambda v=v: to_right(v).wait_send())
         pl.when(has_left)(lambda: to_left().wait_send())
 
     return finish
@@ -300,58 +329,70 @@
     stats[...] = jnp.sum(row, axis=0, keepdims=True)
 
 
+def volume_pass(
+    depth_total, depth_local, picked, first, last, feats, shifts, frame, slab, sum_one, sum_two
+):
+    views, high, n = feats.shape
+    n = n - LANES
+    channels = high // ROWS
+    first_depth = lax.axis_index("depth") * depth_local
+    first_col = lax.axis_index("col") * n
+    lane = iota((ROWS, LANES), 1)
+    pair_lane = iota((2 * ROWS, LANES), 1)
+
+    def one_depth(step, _):
+        depth = first_depth + step - 1
+        valid = (depth >= 0) & (depth < depth_total)
+        clipped = jnp.clip(depth, 0, depth_total - 1)
+        moves = [shifts[v, clipped] for v in picked]
+        wraps = [pair_lane >= LANES - move for move in moves]
+        for j in range(n // LANES):
+            here = slice(j * LANES, (j + 1) * LANES)
+            if last:
+                x = first_col + j * LANES + lane
+                tally = jnp.zeros((ROWS, LANES), f32)
+                for v in range(views):
+                    c = x - shifts[v, clipped]
+                    mask = (c >= frame[0, v]) & (c < frame[1, v])
+                    tally = tally + jnp.where(mask, 1.0, 0.0)
+                scale = 1.0 / tally
+                last_scale = jnp.where(valid, scale, 0.0)
+                scale, last_scale = [
+                    jnp.concatenate([part, part], axis=0) for part in (scale, last_scale)
+                ]
+            for pair in range(channels // 2):
+                rows = slice(pair * 2 * ROWS, (pair + 1) * 2 * ROWS)
+                where_to = pl.ds(pl.multiple_of(step * high + pair * 2 * ROWS, 2 * ROWS), 2 * ROWS)
+                ones, twos = [], []
+                if not first:
+                    ones.append(sum_one[where_to, here])
+                    twos.append(sum_two[where_to, here])
+                for v, move, wrap in zip(picked, moves, wraps):
+                    value = feats[v, rows, (j + 1) * LANES : (j + 2) * LANES]
+                    behind = feats[v, rows, here]
+                    value = pltpu.roll(jnp.where(wrap, behind, value), move, 1).astype(f32)
+                    ones.append(value)
+                    twos.append(value * value)
+                total, square = tree_sum(ones), tree_sum(twos)
+                if last:
+                    square = jnp.maximum(square - total * (total * scale), 0.0) * last_scale
+                    slab[where_to, here] = square.astype(bf16)
+                else:
+                    sum_one[where_to, here] = total
+                    sum_two[where_to, here] = square
+        return _
+
+    lax.fori_loop(0, depth_local + 2, one_depth, 0, unroll=2)
+
+
 def volume_stage(
     depth_total, depth_local, cols, own, left, right, edge, feats, shifts, frame, shift_rows, mat, out,
-    pack_left, pack_right, stats, slab
+    pack_left, pack_right, stats, slab, sum_one, sum_two
 ):
     views, high, n = own.shape
     channels = high // ROWS
     first_depth = lax.axis_index("depth") * depth_local
     first_col = lax.axis_index("col") * n
-    lane = iota((ROWS, LANES), 1)
-    pair_lane = iota((2 * ROWS, LANES), 1)
-
-    def one_depth(step, _):
-        depth = first_depth + step - 1
-        valid = (depth >= 0) & (depth < depth_total)
-        clipped = jnp.clip(depth, 0, depth_total - 1)
-        moves = [shifts[v, clipped] for v in range(views)]
-        for j in range(n // LANES):
-            x = first_col + j * LANES + lane
-            wraps = []
-            tally = jnp.zeros((ROWS, LANES), f32)
-            for v in range(views):
-                c = x - moves[v]
-                mask = (c >= frame[0, v]) & (c < frame[1, v])
-                tally = tally + jnp.where(mask, 1.0, 0.0)
-                wraps.append(pair_lane >= LANES - moves[v])
-            scale = 1.0 / tally
-            last_scale = jnp.where(valid, scale, 0.0)
-            scale, last_scale = [
-                jnp.concatenate([part, part], axis=0) for part in (scale, last_scale)
-            ]
-
-            def one_pair(pair, _):
-                rows = pl.ds(pl.multiple_of(pair * 2 * ROWS, 2 * ROWS), 2 * ROWS)
-                vals = []
-                for v in range(views):
-                    value = feats[v, rows, (j + 1) * LANES : (j + 2) * LANES]
-                    if v:
-                        behind = feats[v, rows, j * LANES : (j + 1) * LANES]
-                        value = pltpu.roll(jnp.where(wraps[v], behind, value), moves[v], 1)
-                    vals.append(value.astype(f32))
-                total = tree_sum(vals)
-                square = tree_sum([value * value for value in vals])
-                square = jnp.maximum(square - total * (total * scale), 0.0) * last_scale
-                where_to = pl.ds(pl.multiple_of(step * high + pair * 2 * ROWS, 2 * ROWS), 2 * ROWS)
-                slab[where_to, j * LANES : (j + 1) * LANES] = square.astype(bf16)
-                return _
-
-            lax.fori_loop(0, channels // 2, one_pair, 0, unroll=True)
-        return _
-
-    lax.fori_loop(0, depth_local + 2, one_depth, 0, unroll=2)
-
     view_lane = iota(right.shape, 1)
     ahead = jnp.zeros(right.shape, bf16)
     for v in range(views):
@@ -595,8 +636,15 @@
     def all_known():
         pl.semaphore_wait(known_sem, cols - 1)
 
+    feats = gathered[4]
+
+    def run_pass(picked, first_pass, last_pass):
+        volume_pass(
+            depth_total, depth_local, picked, first_pass, last_pass, feats, shifts, frame, *volume_refs
+        )
+
     sent = feature_stage(
-        depths, cols, ready, raw_views, feat_weight, cost_weight, mid_weight, final_weight, frame,
+        depths, cols, ready, run_pass, raw_views, feat_weight, cost_weight, mid_weight, final_weight, frame,
         *gathered, *mats, *feature_refs
     )
     volume_stage(
@@ -652,10 +700,12 @@
         buffer((high, LANES), bf16),
         buffer((view_local, high, n), f32),
         buffer((3 * high, high), bf16),
-        dma(2), dma(2), dma(views), dma(views), dma(views), dma(views), dma(1), dma(1),
+        dma(2), dma(2), dma(views + depths), dma(views), dma(views), dma(views), dma(1), dma(1),
     ]
     volume_refs = [
         buffer(((depth_local + 2) * high, n), bf16),
+        buffer(((depth_local + 2) * high, n), f32),
+        buffer(((depth_local + 2) * high, n), f32),
     ]
 
     def conv_refs():
@@ -694,7 +744,7 @@
         in_specs=[vmem] * 5 + [smem] * 2 + [vmem],
         out_specs=vmem,
         scratch_shapes=[ref for g in groups for ref in g],
-        compiler_params=pltpu.CompilerParams(collective_id=0, has_side_effects=True),
+        compiler_params=pltpu.CompilerParams(collective_id=0, has_side_effects=True, vmem_limit_bytes=40 * 2**20),
         name="whole",
     )(
         raw_views, feat_weight, cost_weight, jnp.transpose(mid_weight, (1, 2, 0)),

time: 50.8 us -> 51.5 us (1.014)
  local copies, waits for them, and re-layouts: 1.28 us -> 5.29 us
  Pallas kernels: 49.3 us -> 45.8 us
    unnamed x1 -> x15, local copies, waits for them, and re-layouts: 1.28 us -> 5.29 us
    pallas_call x1, Pallas kernels: 49.3 us -> 45.8 us  [local(): pl.pallas_call(functools.partial(whole_kernel, [len(g) for g in groups],...]
where the time goes in v3:
time: 51.5 us; the launch traced here: 51.1 us
  Pallas kernels  45.8 us (89%)
  local copies, waits for them, and re-layouts  5.29 us (10%)
    pallas_call x1, Pallas kernels, local(): pl.pallas_call(functools.partial(whole_kernel, [len(g) for g in groups],...  45.8 us
    unnamed x15, local copies, waits for them, and re-layouts  5.29 us

profile of v3, /device:TPU:0, one launch (start us, length us, event | category | flops | bytes accessed | tf_op | source)
XLA Modules:
  0.0 51.1 jit_solution(6095186242046100292)
XLA Ops:
  0.0 0.0 copy-start.3
  0.0 0.0 copy-start.6
  0.0 0.7 %copy-done.3 = s32[8,96]{1,0:T(8,128)S(1)} copy-done((s32[8,96]{1,0:T(8,128)S(1)}, s32[8,96]{1,0:T(8,128)}, u32[]{:S(2)}) %copy-start.3) | copy-done | bytes 3096
  0.7 0.0 copy-done.6
  0.7 0.0 copy-start
  0.7 0.9 %copy-done = bf16[2,32,8,128]{3,2,1,0:T(8,128)(2,1)S(1)} copy-done((bf16[2,32,8,128]{3,2,1,0:T(8,128)(2,1)S(1)}, bf16[2,32,8,128]{3,2,1,0:T(8,128)(2,1)}, u32[]{:S(2)}) %copy-start) | copy-done | bytes 131096
  1.6 0.0 copy-start.1
  1.6 0.9 %copy-done.1 = bf16[9,32,32]{2,1,0:T(8,128)(2,1)S(1)} copy-done((bf16[9,32,32]{2,1,0:T(8,128)(2,1)S(1)}, bf16[9,32,32]{2,1,0:T(8,128)(2,1)}, u32[]{:S(2)}) %copy-start.1) | copy-done | bytes 18456
  2.5 0.0 copy-start.2
  2.5 0.8 %copy-done.2 = bf16[27,8,32]{2,1,0:T(8,128)(2,1)S(1)} copy-done((bf16[27,8,32]{2,1,0:T(8,128)(2,1)S(1)}, bf16[27,8,32]{2,1,0:T(8,128)(2,1)}, u32[]{:S(2)}) %copy-start.2) | copy-done | bytes 13848
  3.3 0.0 copy-start.4
  3.3 0.7 %copy-done.4 = bf16[27,8,8]{0,2,1:T(8,128)(2,1)S(1)} copy-done((bf16[27,8,8]{0,2,1:T(8,128)(2,1)S(1)}, bf16[27,8,8]{0,2,1:T(8,128)(2,1)}, u32[]{:S(2)}) %copy-start.4) | copy-done | bytes 3480
  4.0 0.0 copy-start.5
  4.0 0.7 %copy-done.5 = bf16[27,8]{0,1:T(8,128)(2,1)S(1)} copy-done((bf16[27,8]{0,1:T(8,128)(2,1)S(1)}, bf16[27,8]{0,1:T(8,128)(2,1)}, u32[]{:S(2)}) %copy-start.5) | copy-done | bytes 456
  4.7 45.8 %whole.1 = f32[8,128]{1,0:T(8,128)S(1)} custom-call(bf16[2,32,8,128]{3,2,1,0:T(8,128)(2,1)S(1)} %copy-done, bf16[9,32,32]{2,1,0:T(8,128)(2,1)S(1)} %copy-done.1, bf16[27,8,32]{2,1,0:T(8,128)(2,1)S(1)} %copy-done.2, bf16[8,8,27]{2,1,0:T(8,128)(2,1)S(1)} %bitcast.5, bf16[1,8,27]{2,1,0:T(8,128)(2,1)S(1)} %bitcast.6, s32[8,96]{1,0:T(8,128)S(1)} %copy-done.3, ...), custom_call_target="tpu_custom_call" | custom-call | tf_op jit(solution)/shard_map/whole/pallas_call | solution.py:739
  50.5 0.6 %copy.9 = f32[8,128]{1,0:T(8,128)} copy(f32[8,128]{1,0:T(8,128)S(1)} %whole.1) | data formatting | bytes 8192
Async XLA Ops:
  0.0 0.7 %copy-start.3 = (s32[8,96]{1,0:T(8,128)S(1)}, s32[8,96]{1,0:T(8,128)}, u32[]{:S(2)}) copy-start(s32[8,96]{1,0:T(8,128)} %refs_7_.1) | copy-start | bytes 9220
  0.0 0.7 %copy-start.6 = (s32[8,2]{0,1:T(2,128)S(1)}, s32[8,2]{0,1:T(2,128)}, u32[]{:S(2)}) copy-start(s32[8,2]{0,1:T(2,128)} %param.10) | copy-start | bytes 196
  0.7 0.9 %copy-start = (bf16[2,32,8,128]{3,2,1,0:T(8,128)(2,1)S(1)}, bf16[2,32,8,128]{3,2,1,0:T(8,128)(2,1)}, u32[]{:S(2)}) copy-start(bf16[2,32,8,128]{3,2,1,0:T(8,128)(2,1)} %refs_0_.1) | copy-start | bytes 393220
  1.6 0.9 %copy-start.1 = (bf16[9,32,32]{2,1,0:T(8,128)(2,1)S(1)}, bf16[9,32,32]{2,1,0:T(8,128)(2,1)}, u32[]{:S(2)}) copy-start(bf16[9,32,32]{2,1,0:T(8,128)(2,1)} %refs_1_.1) | copy-start | bytes 55300
  2.5 0.8 %copy-start.2 = (bf16[27,8,32]{2,1,0:T(8,128)(2,1)S(1)}, bf16[27,8,32]{2,1,0:T(8,128)(2,1)}, u32[]{:S(2)}) copy-start(bf16[27,8,32]{2,1,0:T(8,128)(2,1)} %refs_2_.1) | copy-start | bytes 41476
  3.3 0.7 %copy-start.4 = (bf16[27,8,8]{0,2,1:T(8,128)(2,1)S(1)}, bf16[27,8,8]{0,2,1:T(8,128)(2,1)}, u32[]{:S(2)}) copy-start(bf16[27,8,8]{0,2,1:T(8,128)(2,1)} %param.12) | copy-start | bytes 10372
  4.0 0.7 %copy-start.5 = (bf16[27,8]{0,1:T(8,128)(2,1)S(1)}, bf16[27,8]{0,1:T(8,128)(2,1)}, u32[]{:S(2)}) copy-start(bf16[27,8]{0,1:T(8,128)(2,1)} %param.13) | copy-start | bytes 1300

commit v4 on v3

--- a/solution.py
+++ b/solution.py
@@ -13,7 +13,7 @@
 bf16 = jnp.bfloat16
 MESH = pl.DeviceIdType.MESH
 vmem = pl.BlockSpec(memory_space=pltpu.VMEM)
-smem = pl.BlockSpec(memory_space=pltpu.SMEM)
+hbm = pl.BlockSpec(memory_space=pltpu.HBM)
 
 
 def dot(a, b):
@@ -103,7 +103,7 @@
 
 
 def feature_stage(
-    depths, cols, ready, run_pass, raw_views, feat_weight, cost_weight, mid_weight, final_weight, frame, own, left,
+    depths, cols, ready, loaded, run_pass, raw_views, feat_weight, cost_weight, mid_weight, final_weight, frame, own, left,
     right, edge, feats, cost_mat, mid_mat, final_mat, raw, table, cost_table, mid_table, final_table,
     rim, rim_left, rim_right, partial, mat, s_raw, r_raw, s_dep, r_dep, s_right, r_right, s_left, r_left
 ):
@@ -132,6 +132,7 @@
 
     pl.when(has_right)(lambda: edge_right().start())
     pl.when(has_left)(lambda: edge_left().start())
+    loaded()
     expand(feat_weight, table, False)
     bands = row_bands(high)
     for e in range(3):
@@ -225,17 +226,17 @@
         run_pass([at[k][j] for k, j in groups[index]], index == 0, index == len(groups) - 1)
 
     take(groups[0])
-    take(groups[1])
-    use(0)
-    for group in groups[2:]:
+    for index, group in enumerate(groups[1:]):
         take(group)
+        if index < len(groups) - 2:
+            use(index)
     packed = jnp.zeros((high, LANES), bf16)
     for v in range(views):
         first = own[v, :, 0:LANES]
         packed = jnp.where(lane == v, pltpu.roll(first, v, 1) if v else first, packed)
     edge[...] = packed
     pl.when(has_left)(lambda: to_left().start())
-    for index in range(1, len(groups)):
+    for index in range(len(groups) - 2, len(groups)):
         use(index)
     pl.when(has_right)(lambda: to_left().wait_recv())
 
@@ -308,7 +309,7 @@
     wide_zero = jnp.zeros((high, n), f32)
     lane_zero = jnp.zeros((high, LANES), f32)
     first, second, pack_l, pack_r = lax.fori_loop(
-        0, half, one_step, (wide_zero, wide_zero, lane_zero, lane_zero), unroll=2
+        0, half, one_step, (wide_zero, wide_zero, lane_zero, lane_zero), unroll=6
     )
     pack_left[...] = pack_l
     pack_right[...] = pack_r
@@ -382,7 +383,7 @@
                     sum_two[where_to, here] = square
         return _
 
-    lax.fori_loop(0, depth_local + 2, one_depth, 0, unroll=2)
+    lax.fori_loop(0, depth_local + 2, one_depth, 0, unroll=(depth_local + 2) // 2)
 
 
 def volume_stage(
@@ -599,15 +600,25 @@
 
 
 def whole_kernel(groups, depths, cols, voxels, depth_total, depth_local, *refs):
-    (
-        raw_views, feat_weight, cost_weight, mid_weight, final_weight, shifts, frame, shift_rows, out
-    ) = refs[:9]
-    rest, taken = [], 9
+    sources, out = refs[:7], refs[7]
+    rest, taken = [], 8
     for size in groups:
         rest.append(refs[taken : taken + size])
         taken += size
-    gathered, mats, feature_refs, volume_refs, first, second, swap_a, swap_b, score_refs, known = rest
+    (
+        gathered, mats, feature_refs, volume_refs, first, second, swap_a, swap_b, score_refs, known,
+        staged
+    ) = rest
     known_sem = known[0]
+    *targets, shift_rows, s_in = staged
+    raw_views, feat_weight, cost_weight, mid_weight, final_weight, shifts, frame = targets
+    pairs = list(zip(sources, targets)) + [(sources[5], shift_rows)]
+    loads = [
+        pltpu.make_async_copy(source, target, s_in.at[i])
+        for i, (source, target) in enumerate(pairs)
+    ]
+    for load in loads:
+        load.start()
     me, col = lax.axis_index("depth"), lax.axis_index("col")
     has_left, has_right = col > 0, col < cols - 1
     has_low, has_high = me > 0, me < depths - 1
@@ -637,6 +648,11 @@
         pl.semaphore_wait(known_sem, cols - 1)
 
     feats = gathered[4]
+    loads[0].wait()
+
+    def loaded():
+        for load in loads[1:]:
+            load.wait()
 
     def run_pass(picked, first_pass, last_pass):
         volume_pass(
@@ -644,8 +660,8 @@
         )
 
     sent = feature_stage(
-        depths, cols, ready, run_pass, raw_views, feat_weight, cost_weight, mid_weight, final_weight, frame,
-        *gathered, *mats, *feature_refs
+        depths, cols, ready, loaded, run_pass, raw_views, feat_weight, cost_weight, mid_weight,
+        final_weight, frame, *gathered, *mats, *feature_refs
     )
     volume_stage(
         depth_total, depth_local, cols, *gathered, shifts, frame, shift_rows, mats[0], *first,
@@ -732,24 +748,28 @@
         buffer((depths, 3, rows, n), f32),
         dma(depths), dma(depths),
     ]
+    operands = [
+        raw_views, feat_weight, cost_weight, jnp.transpose(mid_weight, (1, 2, 0)),
+        jnp.transpose(final_weight)[None], shifts, jnp.transpose(frame_range)
+    ]
     groups = [
         gathered, mats, feature_refs, volume_refs, conv_refs(), conv_refs(), swap_refs(), swap_refs(),
         score_refs, [pltpu.SemaphoreType.REGULAR],
+        [buffer(a.shape, a.dtype) for a in operands[:5]]
+        + [pltpu.SMEM(a.shape, a.dtype) for a in operands[5:]]
+        + [buffer(shifts.shape, jnp.int32), dma(8)],
     ]
     return pl.pallas_call(
         functools.partial(
             whole_kernel, [len(g) for g in groups], depths, cols, voxels, depth_total, depth_local
         ),
         out_shape=jax.ShapeDtypeStruct((rows, n), f32),
-        in_specs=[vmem] * 5 + [smem] * 2 + [vmem],
+        in_specs=[hbm] * 7,
         out_specs=vmem,
         scratch_shapes=[ref for g in groups for ref in g],
-        compiler_params=pltpu.CompilerParams(collective_id=0, has_side_effects=True, vmem_limit_bytes=40 * 2**20),
+        compiler_params=pltpu.CompilerParams(collective_id=0, has_side_effects=True),
         name="whole",
-    )(
-        raw_views, feat_weight, cost_weight, jnp.transpose(mid_weight, (1, 2, 0)),
-        jnp.transpose(final_weight)[None], shifts, jnp.transpose(frame_range), shifts
-    )
+    )(*operands)
 
 
 def solution(mesh):

time: 51.5 us -> 44.1 us (0.86)
  local copies, waits for them, and re-layouts: 5.29 us -> 1.28 us
  Pallas kernels: 45.8 us -> 42.7 us
    unnamed x15 -> x1, local copies, waits for them, and re-layouts: 5.29 us -> 1.28 us
    pallas_call x1, Pallas kernels: 45.8 us -> 42.7 us  [local(): pl.pallas_call(functools.partial(whole_kernel, [len(g) for g in groups],...]
where the time goes in v4:
time: 44.1 us; the launch traced here: 43.9 us
  Pallas kernels  42.7 us (97%)
  local copies, waits for them, and re-layouts  1.28 us (3%)
    pallas_call x1, Pallas kernels, local(): pl.pallas_call(functools.partial(whole_kernel, [len(g) for g in groups],...  42.7 us
    unnamed x1, local copies, waits for them, and re-layouts  1.28 us

profile of v4, /device:TPU:0, one launch (start us, length us, event | category | flops | bytes accessed | tf_op | source)
XLA Modules:
  0.0 43.9 jit_solution(13927116544678472229)
XLA Ops:
  0.0 42.7 %whole.1 = f32[8,128]{1,0:T(8,128)} custom-call(bf16[2,32,8,128]{3,2,1,0:T(8,128)(2,1)} %refs_0_.1, bf16[9,32,32]{2,1,0:T(8,128)(2,1)} %refs_1_.1, bf16[27,8,32]{2,1,0:T(8,128)(2,1)} %refs_2_.1, bf16[8,8,27]{2,1,0:T(8,128)(2,1)} %bitcast.5, bf16[1,8,27]{2,1,0:T(8,128)(2,1)} %bitcast.6, s32[8,96]{1,0:T(8,128)} %refs_5_.1, s32[2,8]{1,0:T(2,128)} %bitcast.7), custom_call_target="tpu_custom_call" | custom-call | tf_op jit(solution)/shard_map/whole/pallas_call | solution.py:762
  42.7 1.3 %copy.9 = f32[8,128]{1,0:T(8,128)} copy(f32[8,128]{1,0:T(8,128)} %whole.1) | data formatting | bytes 8192

commit v5 on v4

--- a/solution.py
+++ b/solution.py
@@ -103,7 +103,8 @@
 
 
 def feature_stage(
-    depths, cols, ready, loaded, run_pass, raw_views, feat_weight, cost_weight, mid_weight, final_weight, frame, own, left,
+    depths, cols, ready, loaded, prepare, run_pass, raw_views, feat_weight, cost_weight, mid_weight,
+    final_weight, frame, own, left,
     right, edge, feats, cost_mat, mid_mat, final_mat, raw, table, cost_table, mid_table, final_table,
     rim, rim_left, rim_right, partial, mat, s_raw, r_raw, s_dep, r_dep, s_right, r_right, s_left, r_left
 ):
@@ -225,6 +226,7 @@
             absorb(v, left, 0, LANES)
         run_pass([at[k][j] for k, j in groups[index]], index == 0, index == len(groups) - 1)
 
+    prepare()
     take(groups[0])
     for index, group in enumerate(groups[1:]):
         take(group)
@@ -304,12 +306,12 @@
         return tuple(carry)
 
     if stats is None:
-        lax.fori_loop(0, half, one_step, (), unroll=4)
+        lax.fori_loop(0, half, one_step, (), unroll=12)
         return
     wide_zero = jnp.zeros((high, n), f32)
     lane_zero = jnp.zeros((high, LANES), f32)
     first, second, pack_l, pack_r = lax.fori_loop(
-        0, half, one_step, (wide_zero, wide_zero, lane_zero, lane_zero), unroll=6
+        0, half, one_step, (wide_zero, wide_zero, lane_zero, lane_zero), unroll=12
     )
     pack_left[...] = pack_l
     pack_right[...] = pack_r
@@ -330,15 +332,31 @@
     stats[...] = jnp.sum(row, axis=0, keepdims=True)
 
 
+def count_views(depth_total, depth_local, shifts, frame, scales):
+    views = shifts.shape[0]
+    n = scales.shape[2]
+    first_depth = lax.axis_index("depth") * depth_local
+    x = lax.axis_index("col") * n + iota((ROWS, n), 1)
+
+    def one_depth(step, _):
+        clipped = jnp.clip(first_depth + step - 1, 0, depth_total - 1)
+        tally = jnp.zeros((ROWS, n), f32)
+        for v in range(views):
+            c = x - shifts[v, clipped]
+            tally = tally + jnp.where((c >= frame[0, v]) & (c < frame[1, v]), 1.0, 0.0)
+        scales[step] = 1.0 / tally
+        return _
+
+    lax.fori_loop(0, depth_local + 2, one_depth, 0, unroll=2)
+
+
 def volume_pass(
-    depth_total, depth_local, picked, first, last, feats, shifts, frame, slab, sum_one, sum_two
+    depth_total, depth_local, picked, first, last, feats, shifts, slab, sum_one, sum_two, scales
 ):
     views, high, n = feats.shape
     n = n - LANES
     channels = high // ROWS
     first_depth = lax.axis_index("depth") * depth_local
-    first_col = lax.axis_index("col") * n
-    lane = iota((ROWS, LANES), 1)
     pair_lane = iota((2 * ROWS, LANES), 1)
 
     def one_depth(step, _):
@@ -350,17 +368,8 @@
         for j in range(n // LANES):
             here = slice(j * LANES, (j + 1) * LANES)
             if last:
-                x = first_col + j * LANES + lane
-                tally = jnp.zeros((ROWS, LANES), f32)
-                for v in range(views):
-                    c = x - shifts[v, clipped]
-                    mask = (c >= frame[0, v]) & (c < frame[1, v])
-                    tally = tally + jnp.where(mask, 1.0, 0.0)
-                scale = 1.0 / tally
+                scale = jnp.concatenate([scales[step, :, here]] * 2, axis=0)
                 last_scale = jnp.where(valid, scale, 0.0)
-                scale, last_scale = [
-                    jnp.concatenate([part, part], axis=0) for part in (scale, last_scale)
-                ]
             for pair in range(channels // 2):
                 rows = slice(pair * 2 * ROWS, (pair + 1) * 2 * ROWS)
                 where_to = pl.ds(pl.multiple_of(step * high + pair * 2 * ROWS, 2 * ROWS), 2 * ROWS)
@@ -388,7 +397,7 @@
 
 def volume_stage(
     depth_total, depth_local, cols, own, left, right, edge, feats, shifts, frame, shift_rows, mat, out,
-    pack_left, pack_right, stats, slab, sum_one, sum_two
+    pack_left, pack_right, stats, slab, sum_one, sum_two, scales
 ):
     views, high, n = own.shape
     channels = high // ROWS
@@ -534,7 +543,7 @@
         )
         return _
 
-    lax.fori_loop(0, depth_local, one_plane, 0, unroll=2)
+    lax.fori_loop(0, depth_local, one_plane, 0, unroll=8)
     lane = iota((high, LANES), 1)
     halos = []
     for parts, ok in ((from_left, has_left), (from_right, has_right)):
@@ -654,13 +663,16 @@
         for load in loads[1:]:
             load.wait()
 
+    def prepare():
+        count_views(depth_total, depth_local, shifts, frame, volume_refs[3])
+
     def run_pass(picked, first_pass, last_pass):
         volume_pass(
-            depth_total, depth_local, picked, first_pass, last_pass, feats, shifts, frame, *volume_refs
+            depth_total, depth_local, picked, first_pass, last_pass, feats, shifts, *volume_refs
         )
 
     sent = feature_stage(
-        depths, cols, ready, loaded, run_pass, raw_views, feat_weight, cost_weight, mid_weight,
+        depths, cols, ready, loaded, prepare, run_pass, raw_views, feat_weight, cost_weight, mid_weight,
         final_weight, frame, *gathered, *mats, *feature_refs
     )
     volume_stage(
@@ -722,6 +734,7 @@
         buffer(((depth_local + 2) * high, n), bf16),
         buffer(((depth_local + 2) * high, n), f32),
         buffer(((depth_local + 2) * high, n), f32),
+        buffer((depth_local + 2, rows, n), f32),
     ]
 
     def conv_refs():
@@ -767,9 +780,11 @@
         in_specs=[hbm] * 7,
         out_specs=vmem,
         scratch_shapes=[ref for g in groups for ref in g],
-        compiler_params=pltpu.CompilerParams(collective_id=0, has_side_effects=True),
+        compiler_params=pltpu.CompilerParams(
+            collective_id=0, has_side_effects=True, vmem_limit_bytes=40 * 2**20
+        ),
         name="whole",
-    )(*operands)
+    )(*[pltpu.with_memory_space_constraint(a, pltpu.HBM) for a in operands])
 
 
 def solution(mesh):

time: 44.1 us -> 41.4 us (0.939)
  Pallas kernels: 42.7 us -> 40.6 us
  local copies, waits for them, and re-layouts: 1.28 us -> 0.6 us
    pallas_call x1, Pallas kernels: 42.7 us -> 40.6 us  [local(): pl.pallas_call(functools.partial(whole_kernel, [len(g) for g in groups],...]
    unnamed x1, local copies, waits for them, and re-layouts: 1.28 us -> 0.6 us
where the time goes in v5:
time: 41.4 us; the launch traced here: 41.2 us
  Pallas kernels  40.6 us (98%)
  local copies, waits for them, and re-layouts  0.6 us (1%)
    pallas_call x1, Pallas kernels, local(): pl.pallas_call(functools.partial(whole_kernel, [len(g) for g in groups],...  40.6 us

profile of v5, /device:TPU:0, one launch (start us, length us, event | category | flops | bytes accessed | tf_op | source)
XLA Modules:
  0.0 41.2 jit_solution(7732739000073318778)
XLA Ops:
  0.0 40.6 %whole.1 = f32[8,128]{1,0:T(8,128)S(1)} custom-call(bf16[2,32,8,128]{3,2,1,0:T(8,128)(2,1)} %refs_0_.1, bf16[9,32,32]{2,1,0:T(8,128)(2,1)} %refs_1_.1, bf16[27,8,32]{2,1,0:T(8,128)(2,1)} %refs_2_.1, bf16[8,8,27]{2,1,0:T(8,128)(2,1)} %bitcast.5, bf16[1,8,27]{2,1,0:T(8,128)(2,1)} %bitcast.6, s32[8,96]{1,0:T(8,128)} %refs_5_.1, s32[2,8]{1,0:T(2,128)} %bitcast.7), custom_call_target="tpu_custom_call" | custom-call | tf_op jit(solution)/shard_map/whole/pallas_call | solution.py:775
  40.6 0.6 %copy.9 = f32[8,128]{1,0:T(8,128)} copy(f32[8,128]{1,0:T(8,128)S(1)} %whole.1) | data formatting | bytes 8192
